TPU v7x, 256 devices: a whole 4x4x8 slice. The times are simulated.
256 devices in a mesh: grp: 4 (over x), ep: 64 (over y, z, core).
Axes of the slice: x: 4, y: 4, z: 8, core: 2. Of those that a mesh axis runs over, the one named last changes fastest.
Arguments:
- queries: bfloat16 [6144, 4096], P(('grp', 'ep')), may hold values from -9 to 9
- new_keys: bfloat16 [6144, 512], P(('grp', 'ep')), may hold values from -9 to 9
- new_values: bfloat16 [6144, 512], P(('grp', 'ep')), may hold values from -6 to 6
- key_cache: bfloat16 [4096, 48, 512], P(('grp', 'ep')), may hold values from -9 to 9
- value_cache: bfloat16 [4096, 48, 512], P(('grp', 'ep')), may hold values from -6 to 6
- cache_len: int32 [4096], P(('grp', 'ep')), may hold values from 2 to 48, as said below
- residual: bfloat16 [6144, 2048], P(('grp', 'ep')), may hold values from -17 to 17
- out_proj: bfloat16 [4096, 2048], P(None, 'grp'), may hold values from -0.09375 to 0.09375
- norm_gain: float32 [2048], P('grp'), may hold values from 0.1 to 1.9
- expert_ids: int32 [6144, 8], P(('grp', 'ep')), may hold values from 0 to 127, as said below
- route_weights: bfloat16 [6144, 8], P(('grp', 'ep')), may hold values from 0.049804688 to 1
- slot_expert: int32 [192], replicated, may hold values from 0 to 127, as said below
- gate_up: bfloat16 [192, 2048, 1536], P('ep', 'grp'), may hold values from -1 to 1, as said below
- down_proj: bfloat16 [192, 768, 2048], P('ep', None, 'grp'), may hold values from -2 to 2, as said below
Outputs:
- moe_out: bfloat16 [6144, 2048], P(('grp', 'ep'))
- layer_out: bfloat16 [6144, 2048], P(('grp', 'ep'))
Inputs may be any that keep to these rules, and one draw needn't show every extreme that they name: `expert_ids`: each row names 8 different experts. In the rows of one device one expert, the same on all devices, is named by exactly 3 rows, and every other expert by at most 2 rows; some expert other than it is named by exactly 2 rows of a device. `slot_expert`: every expert is held by one or two slots; the expert named by 3 rows of every device is held by two. `cache_len`: some request has exactly 48 cached tokens. `gate_up`: slots holding the same expert hold equal weights. `down_proj`: slots holding the same expert hold equal weights.
All inputs are finite; a program needn't handle non-finite values.
Results may differ from a plain program's by a relative error of at most 0.033.
Values may be sent and summed in bfloat16 or wider, within the bound.
A program may use at most 128 MiB of HBM per device.

v0:
```python
import math

import jax
import jax.numpy as jnp
from jax import lax
from jax.sharding import PartitionSpec as P

D = 2048
HEADS = 32
KV_HEADS = 4
HEAD_DIM = 128
FF = 768
TOPK = 8
EXP_DEV = 2
SLOTS_DEV = 3
PRE = 8


masked_score = -1e30
epsilon = 1e-06


def prefill_context(queries, new_keys, new_values):
    head_group = HEADS // KV_HEADS
    scaling = 1.0 / math.sqrt(HEAD_DIM)
    query_pre = queries[:PRE].reshape(PRE, KV_HEADS, head_group, HEAD_DIM)
    keys_pre = new_keys[:PRE].reshape(PRE, KV_HEADS, HEAD_DIM)
    values_pre = new_values[:PRE].reshape(PRE, KV_HEADS, HEAD_DIM)
    scores = (
        jnp.einsum("ikgd,jkd->kgij", query_pre, keys_pre, preferred_element_type=jnp.float32)
        * scaling
    )
    causal = jnp.arange(PRE)[:, None] >= jnp.arange(PRE)[None, :]
    scores = jnp.where(causal, scores, masked_score)
    exponent = jnp.exp(scores - jnp.max(scores, axis=-1, keepdims=True))
    attn_probs = (exponent / jnp.sum(exponent, axis=-1, keepdims=True)).astype(jnp.bfloat16)
    mixed_values = jnp.einsum(
        "kgij,jkd->ikgd", attn_probs, values_pre, preferred_element_type=jnp.float32
    )
    return mixed_values.astype(jnp.bfloat16).reshape(PRE, HEADS * HEAD_DIM)


def decode_context(queries, new_keys, new_values, key_cache, value_cache, cache_len):
    requests = key_cache.shape[0]
    cache_slots = key_cache.shape[1]
    head_group = HEADS // KV_HEADS
    scaling = 1.0 / math.sqrt(HEAD_DIM)
    query_dec = queries[PRE:].reshape(requests, KV_HEADS, head_group, HEAD_DIM)
    keys_dec = new_keys[PRE:].reshape(requests, KV_HEADS, HEAD_DIM)
    values_dec = new_values[PRE:].reshape(requests, KV_HEADS, HEAD_DIM)
    cached_keys = key_cache.reshape(requests, cache_slots, KV_HEADS, HEAD_DIM)
    cached_values = value_cache.reshape(requests, cache_slots, KV_HEADS, HEAD_DIM)
    cache_scores = (
        jnp.einsum("nkgd,ntkd->nkgt", query_dec, cached_keys, preferred_element_type=jnp.float32)
        * scaling
    )
    own_score = (
        jnp.einsum("nkgd,nkd->nkg", query_dec, keys_dec, preferred_element_type=jnp.float32)
        * scaling
    )
    valid = jnp.arange(cache_slots)[None, :] < cache_len[:, None]
    cache_scores = jnp.where(valid[:, None, None, :], cache_scores, masked_score)
    top_score = jnp.maximum(jnp.max(cache_scores, axis=-1), own_score)
    cache_exp = jnp.exp(cache_scores - top_score[..., None])
    own_exp = jnp.exp(own_score - top_score)
    denominator = jnp.sum(cache_exp, axis=-1) + own_exp
    cache_probs = (cache_exp / denominator[..., None]).astype(jnp.bfloat16)
    own_probs = (own_exp / denominator).astype(jnp.bfloat16)
    mixed_values = jnp.einsum(
        "nkgt,ntkd->nkgd", cache_probs, cached_values, preferred_element_type=jnp.float32
    )
    mixed_values = (
        mixed_values
        + own_probs.astype(jnp.float32)[..., None] * values_dec.astype(jnp.float32)[:, :, None, :]
    )
    return mixed_values.astype(jnp.bfloat16).reshape(requests, HEADS * HEAD_DIM)


def activate(summed):
    return (jax.nn.silu(summed[..., :FF]) * summed[..., FF:]).astype(jnp.bfloat16)


def local(
    queries,
    new_keys,
    new_values,
    key_cache,
    value_cache,
    cache_len,
    residual,
    out_proj,
    norm_gain,
    expert_ids,
    route_weights,
    slot_expert,
    gate_up,
    down_proj,
):
    rows_dev = queries.shape[0]
    width_part = out_proj.shape[1]
    ep_devices = lax.axis_size("ep")
    group_devices = lax.axis_size("grp")
    experts_all = EXP_DEV * ep_devices
    most_rows = min(rows_dev, (TOPK * rows_dev + experts_all - 2) // (experts_all - 1) + 1)
    context = jnp.concatenate(
        [
            prefill_context(queries, new_keys, new_values),
            decode_context(queries, new_keys, new_values, key_cache, value_cache, cache_len),
        ],
        axis=0,
    )
    context_col, ids_col, weights_col = (
        lax.all_gather(context, "grp", axis=0, tiled=True),
        lax.all_gather(expert_ids, "grp", axis=0, tiled=True),
        lax.all_gather(route_weights, "grp", axis=0, tiled=True),
    )
    residual_col = lax.all_to_all(residual, "grp", split_axis=1, concat_axis=0, tiled=True)
    attended = (
        residual_col.astype(jnp.float32)
        + jnp.dot(context_col, out_proj, preferred_element_type=jnp.float32)
    ).astype(jnp.bfloat16)
    attended_f = attended.astype(jnp.float32)
    sum_squares = lax.psum(jnp.sum(attended_f * attended_f, axis=1), "grp")
    normed = (
        attended_f * lax.rsqrt(sum_squares / D + epsilon)[:, None] * norm_gain[None, :]
    ).astype(jnp.bfloat16)
    route_share = weights_col.astype(jnp.float32)
    route_share = route_share / jnp.sum(route_share, axis=-1, keepdims=True)
    expert_range = jnp.arange(experts_all, dtype=jnp.int32)
    holds = slot_expert[None, :] == expert_range[:, None]
    first_slot = jnp.argmax(holds, axis=1)
    picked = (ids_col[:, :, None] == expert_range[None, None, :]).astype(jnp.int32)
    first_of = jnp.sum(picked * first_slot[None, None, :], axis=-1)
    per_row = jnp.sum(picked, axis=1)
    before = jnp.cumsum(per_row, axis=0) - per_row
    ranking = jnp.sum(picked * before[:, None, :], axis=-1)
    capacity = group_devices * most_rows
    target_dev = first_of // SLOTS_DEV
    local_slot = first_of % SLOTS_DEV
    flat_index = (target_dev * capacity + ranking) * SLOTS_DEV + local_slot
    column_rows = normed.shape[0]
    sources = jnp.broadcast_to(normed[:, None, :], (column_rows, TOPK, width_part)).reshape(
        column_rows * TOPK, width_part
    )
    outgoing = (
        jnp.zeros((ep_devices * capacity * SLOTS_DEV, width_part), jnp.bfloat16)
        .at[flat_index.reshape(-1)]
        .set(sources)
    )
    received = lax.all_to_all(
        outgoing.reshape(ep_devices, capacity * SLOTS_DEV, width_part),
        "ep",
        split_axis=0,
        concat_axis=0,
        tiled=True,
    )
    received = received.reshape(ep_devices * capacity, SLOTS_DEV, width_part)
    partial_term = jnp.einsum("rsd,sdf->rsf", received, gate_up, preferred_element_type=jnp.float32)
    summed = lax.psum(partial_term.astype(jnp.bfloat16), "grp").astype(jnp.float32)
    hidden = activate(summed)
    expert_out = jnp.einsum(
        "rsh,shd->rsd", hidden, down_proj, preferred_element_type=jnp.float32
    ).astype(jnp.bfloat16)
    returned = lax.all_to_all(
        expert_out.reshape(ep_devices, capacity * SLOTS_DEV, width_part),
        "ep",
        split_axis=0,
        concat_axis=0,
        tiled=True,
    )
    returned = returned.reshape(ep_devices * capacity * SLOTS_DEV, width_part)
    gathered = returned[flat_index]
    mixture = jnp.sum(route_share[:, :, None] * gathered.astype(jnp.float32), axis=1)
    moe_col = mixture.astype(jnp.bfloat16)
    layer_col = (attended_f + mixture).astype(jnp.bfloat16)
    moe_out, layer_out = (
        lax.all_to_all(moe_col, "grp", split_axis=0, concat_axis=1, tiled=True),
        lax.all_to_all(layer_col, "grp", split_axis=0, concat_axis=1, tiled=True),
    )
    return (moe_out, layer_out)


def solution(mesh):
    placed = (
        P(("grp", "ep"), None),
        P(("grp", "ep"), None),
        P(("grp", "ep"), None),
        P(("grp", "ep"), None, None),
        P(("grp", "ep"), None, None),
        P(("grp", "ep")),
        P(("grp", "ep"), None),
        P(None, "grp"),
        P("grp"),
        P(("grp", "ep"), None),
        P(("grp", "ep"), None),
        P(),
        P("ep", "grp", None),
        P("ep", None, "grp"),
    )
    return jax.shard_map(
        local,
        mesh=mesh,
        in_specs=placed,
        out_specs=(P(("grp", "ep"), None), P(("grp", "ep"), None)),
        check_vma=False,
    )
```

profile of v0, /device:TPU:32, one launch (start us, length us, event | category | flops | bytes accessed | tf_op | source)
XLA Modules:
  0.0 445.4 jit_solution(7797407101275911876)
XLA Ops:
  8.9 4.3 all-to-all-start
  15.0 12.9 %all-gather.1 = s32[4,24,8]{1,2,0:T(8,128)S(1)} all-gather(s32[1,24,8]{1,2,0:T(8,128)} %bitcast.142), channel_id=1, replica_groups=mesh['grp'=4,'ep'=64] {'grp'}, dimensions={0}, use_global_device_ids=true | all-gather | bytes 3840 | tf_op jit(solution)/shard_map/all_gather | solution.py:114
  29.6 3.4 select_reduce_fusion
  40.1 13.9 %all_gather.11 = bf16[96,4096]{1,0:T(8,128)(2,1)S(1)} all-gather(bf16[24,4096]{1,0:T(8,128)(2,1)S(1)} %pad_maximum_fusion), channel_id=1, replica_groups=mesh['grp'=4,'ep'=64] {'grp'}, dimensions={0}, use_global_device_ids=true | all-gather | bytes 983040 | tf_op jit(solution)/shard_map/all_gather | solution.py:113
  54.4 3.1 multiply_reduce_fusion
  57.5 10.1 %psum.14 = f32[96]{0:T(128)S(1)} all-reduce(f32[96]{0:T(128)S(1)} %get-tuple-element.18), channel_id=1, replica_groups=mesh['grp'=4,'ep'=64] {'grp'}, use_global_device_ids=true, to_apply=%region_11.12 | all-reduce | flops 96 | bytes 768 | tf_op jit(solution)/shard_map/psum | solution.py:123
  67.7 7.4 %scatter_custom_fusion = bf16[2304,512]{1,0:T(8,128)(2,1)} fusion(s32[768]{0:T(1024)S(1)} %fusion.44, bf16[]{:T(256)} %constant.21.clone.1, bf16[96,512]{1,0:T(8,128)(2,1)S(1)} %multiply_convert_fusion), kind=kCustom, calls=%fused_computation.11 | custom fusion | bytes 2457602 | tf_op jit(solution)/shard_map/scatter | solution.py:148
  75.1 4.7 %reshape.281 = bf16[64,36,512]{2,1,0:T(8,128)(2,1)} reshape(bf16[2304,512]{1,0:T(8,128)(2,1)} %scatter_custom_fusion) | data formatting | bytes 4718592 | tf_op jit(solution)/shard_map/reshape | solution.py:151
  79.8 73.8 %all_to_all.58 = bf16[64,36,512]{2,1,0:T(8,128)(2,1)} all-to-all(bf16[64,36,512]{2,1,0:T(8,128)(2,1)} %reshape.281), channel_id=1, replica_groups=mesh['grp'=4,'ep'=64] {'ep'}, dimensions={0} | all-to-all | bytes 4718592 | tf_op jit(solution)/shard_map/all_to_all | solution.py:150
  153.6 6.6 %reshape.282 = bf16[768,3,512]{2,1,0:T(4,128)(2,1)} reshape(bf16[64,36,512]{2,1,0:T(8,128)(2,1)} %all_to_all.58) | data formatting | bytes 4718592 | tf_op jit(solution)/shard_map/reshape | solution.py:157
  160.2 10.0 %convert_bitcast_fusion = bf16[768,3,1536]{2,0,1:T(8,128)(2,1)} fusion(bf16[3,512,1536]{2,1,0:T(8,128)(2,1)} %param.26, bf16[768,3,512]{2,1,0:T(4,128)(2,1)} %reshape.282), kind=kOutput, calls=%fused_computation.5 | convolution fusion | flops 3627417600 | bytes 14155776 | tf_op jit(solution)/shard_map/rsd,sdf->rsf/dot_general | solution.py:158
  170.2 140.2 %all-reduce.2.cloned.1.call-done = bf16[768,3,1536]{2,0,1:T(8,128)(2,1)} async-done(((bf16[768,3,1536]{2,0,1:T(8,128)(2,1)}), bf16[768,3,1536]{2,0,1:T(8,128)(2,1)}) %all-reduce.2.cloned.1.call-update) | async-done | bytes 7077904 | tf_op jit(solution)/shard_map/psum | solution.py:159
  310.4 10.1 %convert_element_type.105 = f32[768,3,1536]{2,0,1:T(8,128)} convert(bf16[768,3,1536]{2,0,1:T(8,128)(2,1)} %all-reduce.2.cloned.1.call-done) | non-fusion elementwise | flops 3538944 | bytes 21233664 | tf_op jit(solution)/shard_map/convert_element_type | solution.py:159
  320.5 7.1 %convert_bitcast_fusion.1 = bf16[768,3,512]{2,0,1:T(8,128)(2,1)S(1)} fusion(bf16[3,768,512]{2,1,0:T(8,128)(2,1)S(1)} %copy-done, f32[768,3,1536]{2,0,1:T(8,128)} %convert_element_type.105), kind=kOutput, calls=%fused_computation.8 | convolution fusion | flops 1823735808 | bytes 18874368 | tf_op jit(solution)/shard_map/rsh,shd->rsd/dot_general | solution.py:161
  327.6 3.7 copy.58
  331.3 6.8 %reshape.283 = bf16[64,36,512]{2,1,0:T(8,128)(2,1)} reshape(bf16[768,3,512]{2,1,0:T(4,128)(2,1)} %copy.58) | data formatting | bytes 4718592 | tf_op jit(solution)/shard_map/reshape | solution.py:165
  338.1 10.8 %all-to-all-start.2 = ((bf16[64,36,512]{2,1,0:T(8,128)(2,1)}), bf16[64,36,512]{2,1,0:T(8,128)(2,1)}, u32[]{:S(2)}, u32[]{:S(2)}) async-start(bf16[64,36,512]{2,1,0:T(8,128)(2,1)} %reshape.283), calls=%async_computation.2 | async-start | bytes 5242880 | tf_op jit(solution)/shard_map/all_to_all | solution.py:164
  349.0 10.4 %all-gather = bf16[4,24,8]{1,2,0:T(8,128)(2,1)S(1)} all-gather(bf16[1,24,8]{1,2,0:T(8,128)(2,1)S(1)} %bitcast.143), channel_id=1, replica_groups=mesh['grp'=4,'ep'=64] {'grp'}, dimensions={0}, use_global_device_ids=true | all-gather | bytes 1920 | tf_op jit(solution)/shard_map/all_gather | solution.py:115
  359.7 49.8 %all-to-all-done.2 = bf16[64,36,512]{2,1,0:T(8,128)(2,1)} async-done(((bf16[64,36,512]{2,1,0:T(8,128)(2,1)}), bf16[64,36,512]{2,1,0:T(8,128)(2,1)}, u32[]{:S(2)}, u32[]{:S(2)}) %all-to-all-start.2) | async-done | bytes 2359328 | tf_op jit(solution)/shard_map/all_to_all | solution.py:164
  409.5 4.9 %reshape.284 = bf16[2304,512]{1,0:T(8,128)(2,1)} reshape(bf16[64,36,512]{2,1,0:T(8,128)(2,1)} %all-to-all-done.2) | data formatting | bytes 4718592 | tf_op jit(solution)/shard_map/reshape | solution.py:171
  414.4 4.7 %gather_fusion = bf16[768,512]{1,0:T(8,128)(2,1)S(1)} fusion(bf16[2304,512]{1,0:T(8,128)(2,1)} %reshape.284, s32[1024]{0:T(1024)S(1)} %pad_clamp_fusion), kind=kCustom, calls=%fused_computation | custom fusion | bytes 1575936 | tf_op jit(solution)/shard_map/gather | solution.py:172
  420.3 8.5 %all_to_all.59 = bf16[4,24,512]{2,1,0:T(8,128)(2,1)S(1)} all-to-all(bf16[4,24,512]{2,1,0:T(8,128)(2,1)S(1)} %bitcast.134), channel_id=1, replica_groups=mesh['grp'=4,'ep'=64] {'grp'}, dimensions={0} | all-to-all | bytes 196608 | tf_op jit(solution)/shard_map/all_to_all | solution.py:177
  428.8 3.3 all-to-all-start.4
  432.8 5.1 %all-to-all-done.4 = bf16[4,24,512]{2,1,0:T(8,128)(2,1)S(1)} async-done(((bf16[4,24,512]{2,1,0:T(8,128)(2,1)}), bf16[4,24,512]{2,1,0:T(8,128)(2,1)S(1)}, u32[]{:S(2)}, u32[]{:S(2)}) %all-to-all-start.4) | async-done | bytes 98336 | tf_op jit(solution)/shard_map/all_to_all | solution.py:178
  (62 shorter events, 15.5 us)
Async XLA Ops:
  7.2 313.4 %copy-start = (bf16[3,768,512]{2,1,0:T(8,128)(2,1)S(1)}, bf16[3,768,512]{2,1,0:T(8,128)(2,1)}, u32[]{:S(2)}) copy-start(bf16[3,768,512]{2,1,0:T(8,128)(2,1)} %param.27) | copy-start | bytes 7077892
  7.2 29.9 %copy-start.2 = (bf16[24,512]{1,0:T(8,128)(2,1)S(1)}, bf16[24,512]{1,0:T(8,128)(2,1)}, u32[]{:S(2)}) copy-start(bf16[24,512]{1,0:T(8,128)(2,1)} %param.16) | copy-start | bytes 73732
  8.9 45.5 %all-to-all-start = ((bf16[24,4,512]{2,0,1:T(8,128)(2,1)}), bf16[24,4,512]{2,0,1:T(8,128)(2,1)S(1)}, u32[]{:S(2)}, u32[]{:S(2)}) async-start(bf16[24,4,512]{2,0,1:T(8,128)(2,1)} %bitcast.125), calls=%async_computation | async-start | bytes 196608 | tf_op jit(solution)/shard_map/all_to_all | solution.py:117
  13.2 297.3 %all-reduce.2.cloned.1.call-start = ((), (), s32[]{:S(2)}) async-start(), calls=%async_computation.5 | async-start | bytes 14155776 | tf_op jit(solution)/shard_map/psum | solution.py:159
  40.1 27.5 %copy-start.3 = (f32[512]{0:T(512)S(1)}, f32[512]{0:T(512)}, u32[]{:S(2)}) copy-start(f32[512]{0:T(512)} %param.22) | copy-start | bytes 6148
  338.1 10.9 %copy-start.4 = (bf16[24,8]{0,1:T(8,128)(2,1)S(1)}, bf16[24,8]{0,1:T(8,128)(2,1)}, u32[]{:S(2)}) copy-start(bf16[24,8]{0,1:T(8,128)(2,1)} %param.24) | copy-start | bytes 1156
  338.1 71.4 %all-to-all-start.2 = ((bf16[64,36,512]{2,1,0:T(8,128)(2,1)}), bf16[64,36,512]{2,1,0:T(8,128)(2,1)}, u32[]{:S(2)}, u32[]{:S(2)}) async-start(bf16[64,36,512]{2,1,0:T(8,128)(2,1)} %reshape.283), calls=%async_computation.2 | async-start | bytes 5242880 | tf_op jit(solution)/shard_map/all_to_all | solution.py:164
  409.5 29.0 %copy-start.1 = (bf16[3,768,512]{2,1,0:T(8,128)(2,1)S(1)}, bf16[3,768,512]{2,1,0:T(8,128)(2,1)}, u32[]{:S(2)}) copy-start(bf16[3,768,512]{2,1,0:T(8,128)(2,1)} %param.27) | copy-start | bytes 7077892
  428.8 9.1 %all-to-all-start.4 = ((bf16[4,24,512]{2,1,0:T(8,128)(2,1)}), bf16[4,24,512]{2,1,0:T(8,128)(2,1)S(1)}, u32[]{:S(2)}, u32[]{:S(2)}) async-start(bf16[4,24,512]{2,1,0:T(8,128)(2,1)} %bitcast.26), calls=%async_computation.4 | async-start | bytes 196608 | tf_op jit(solution)/shard_map/all_to_all | solution.py:178
Sparse Core Ops, SparseCore 0:
  170.4 140.0 all-reduce.1
where the time goes:
time: 448 us; the launch traced here: 445 us
  waiting for transfers between devices  195 us (44%)
  blocking collectives  130 us (29%)
  local copies, waits for them, and re-layouts  45.2 us (10%)
  matrix products  25 us (6%)
  starting transfers between devices  18.4 us (4%)
  other arithmetic  17.7 us (4%)
  between operations  14.3 us (3%)
    psum x1, waiting for transfers between devices, local(): lax.psum(partial_term.astype(jnp.bfloat16), 'grp').astype(jnp.float32)  140 us
    all_to_all x1, blocking collectives, local(): lax.all_to_all(outgoing.reshape(ep_devices, capacity * SLOTS_DEV, width_p...  73.8 us
    all_to_all x1, waiting for transfers between devices, local(): lax.all_to_all(expert_out.reshape(ep_devices, capacity * SLOTS_DEV, width...  49.8 us
    all_gather x1, blocking collectives, local(): lax.all_gather(context, 'grp', axis=0, tiled=True)  13.9 us
    all_gather x1, blocking collectives, local(): lax.all_gather(expert_ids, 'grp', axis=0, tiled=True)  12.9 us
    all_to_all x1, starting transfers between devices, local(): lax.all_to_all(expert_out.reshape(ep_devices, capacity * SLOTS_DEV, width...  10.8 us
    all_gather x1, blocking collectives, local(): lax.all_gather(route_weights, 'grp', axis=0, tiled=True)  10.4 us
    psum x1, blocking collectives, local(): sum_squares = lax.psum(jnp.sum(attended_f * attended_f, axis=1), 'grp')  10.1 us
  transfers between devices with their start and end apart: 4, of which 3 were waited for; matrix products, arithmetic and copies ran while one was open for 3% of the time, Pallas kernels for 0%

commit v1 on v0

--- a/solution.py
+++ b/solution.py
@@ -126,51 +126,51 @@
     ).astype(jnp.bfloat16)
     route_share = weights_col.astype(jnp.float32)
     route_share = route_share / jnp.sum(route_share, axis=-1, keepdims=True)
-    expert_range = jnp.arange(experts_all, dtype=jnp.int32)
-    holds = slot_expert[None, :] == expert_range[:, None]
-    first_slot = jnp.argmax(holds, axis=1)
-    picked = (ids_col[:, :, None] == expert_range[None, None, :]).astype(jnp.int32)
-    first_of = jnp.sum(picked * first_slot[None, None, :], axis=-1)
-    per_row = jnp.sum(picked, axis=1)
-    before = jnp.cumsum(per_row, axis=0) - per_row
-    ranking = jnp.sum(picked * before[:, None, :], axis=-1)
-    capacity = group_devices * most_rows
-    target_dev = first_of // SLOTS_DEV
-    local_slot = first_of % SLOTS_DEV
-    flat_index = (target_dev * capacity + ranking) * SLOTS_DEV + local_slot
     column_rows = normed.shape[0]
-    sources = jnp.broadcast_to(normed[:, None, :], (column_rows, TOPK, width_part)).reshape(
-        column_rows * TOPK, width_part
-    )
-    outgoing = (
-        jnp.zeros((ep_devices * capacity * SLOTS_DEV, width_part), jnp.bfloat16)
-        .at[flat_index.reshape(-1)]
-        .set(sources)
-    )
-    received = lax.all_to_all(
-        outgoing.reshape(ep_devices, capacity * SLOTS_DEV, width_part),
-        "ep",
-        split_axis=0,
-        concat_axis=0,
-        tiled=True,
-    )
-    received = received.reshape(ep_devices * capacity, SLOTS_DEV, width_part)
-    partial_term = jnp.einsum("rsd,sdf->rsf", received, gate_up, preferred_element_type=jnp.float32)
-    summed = lax.psum(partial_term.astype(jnp.bfloat16), "grp").astype(jnp.float32)
-    hidden = activate(summed)
+    slot_rows = 2 * group_devices
+    ep_index = lax.axis_index("ep")
+    ids_all = lax.all_gather(ids_col, "ep", axis=0)
+    share_all = lax.all_gather(route_share, "ep", axis=0)
+    rows_all = lax.all_gather(normed, "ep", axis=0)
+    mine = lax.dynamic_slice_in_dim(slot_expert, ep_index * SLOTS_DEV, SLOTS_DEV)
+    slots = jnp.arange(slot_expert.shape[0], dtype=jnp.int32)
+    same = slot_expert[None, :] == mine[:, None]
+    copies = jnp.sum(same, axis=1)
+    place = ep_index * SLOTS_DEV + jnp.arange(SLOTS_DEV)
+    copy_index = jnp.sum(same & (slots[None, :] < place[:, None]), axis=1)
+    hit = ids_all[:, None, :, :] == mine[None, :, None, None]
+    share = jnp.sum(jnp.where(hit, share_all[:, None, :, :], 0.0), axis=-1)
+    named = jnp.any(hit, axis=-1)
+    count = named.astype(jnp.int32)
+    ranking = jnp.cumsum(count, axis=-1) - count
+    position = ranking // copies[None, :, None]
+    taken = named & (ranking % copies[None, :, None] == copy_index[None, :, None])
+    pick = taken[:, :, None, :] & (
+        position[:, :, None, :] == jnp.arange(slot_rows)[None, None, :, None]
+    )
+    received = jnp.einsum(
+        "sjtr,srd->jstd",
+        pick.astype(jnp.bfloat16),
+        rows_all,
+        preferred_element_type=jnp.float32,
+    ).astype(jnp.bfloat16)
+    received = received.reshape(SLOTS_DEV, ep_devices * slot_rows, width_part)
+    partial_term = jnp.einsum(
+        "jnd,jdf->jnf", received, gate_up, preferred_element_type=jnp.float32
+    ).astype(jnp.bfloat16)
+    summed = lax.psum_scatter(partial_term, "grp", scatter_dimension=1, tiled=True)
+    hidden = activate(summed.astype(jnp.float32))
+    hidden = lax.all_gather(hidden, "grp", axis=1, tiled=True)
     expert_out = jnp.einsum(
-        "rsh,shd->rsd", hidden, down_proj, preferred_element_type=jnp.float32
-    ).astype(jnp.bfloat16)
-    returned = lax.all_to_all(
-        expert_out.reshape(ep_devices, capacity * SLOTS_DEV, width_part),
-        "ep",
-        split_axis=0,
-        concat_axis=0,
-        tiled=True,
-    )
-    returned = returned.reshape(ep_devices * capacity * SLOTS_DEV, width_part)
-    gathered = returned[flat_index]
-    mixture = jnp.sum(route_share[:, :, None] * gathered.astype(jnp.float32), axis=1)
+        "jnh,jhd->jnd", hidden, down_proj, preferred_element_type=jnp.float32
+    ).astype(jnp.bfloat16)
+    expert_out = expert_out.reshape(SLOTS_DEV, ep_devices, slot_rows, width_part)
+    weighted = jnp.where(pick, share[:, :, None, :], 0.0).astype(jnp.bfloat16)
+    mixture = jnp.einsum(
+        "sjtr,jstd->srd", weighted, expert_out, preferred_element_type=jnp.float32
+    ).astype(jnp.bfloat16)
+    mixture = lax.psum_scatter(mixture, "ep", scatter_dimension=0, tiled=False)
+    mixture = mixture.astype(jnp.float32)
     moe_col = mixture.astype(jnp.bfloat16)
     layer_col = (attended_f + mixture).astype(jnp.bfloat16)
     moe_out, layer_out = (

time: 448 us -> 435 us (0.971)
  local copies, waits for them, and re-layouts: 45.2 us -> 6.18 us
  waiting for transfers between devices: 195 us -> 225 us
  blocking collectives: 130 us -> 139 us
  starting transfers between devices: 18.4 us -> 11.9 us
  other arithmetic: 17.7 us -> 12.9 us
    reduce_scatter x0 -> x2, waiting for transfers between devices: none -> 197 us  [the longest x1 146 us: local(): mixture = lax.psum_scatter(mixture, 'ep', scatter_dimension=0, tiled=False)]
    psum x1 -> x0, waiting for transfers between devices: 140 us -> none  [local(): lax.psum(partial_term.astype(jnp.bfloat16), 'grp').astype(jnp.float32)]
    all_gather x0 -> x2, blocking collectives: none -> 91 us  [the longest x1 46.6 us: local(): ids_all = lax.all_gather(ids_col, 'ep', axis=0)]
    all_to_all x2 -> x0, blocking collectives: 82.3 us -> none  [the longest x1 73.8 us: local(): lax.all_to_all(outgoing.reshape(ep_devices, capacity * SLOTS_DEV, width_p...]
    all_to_all x1, waiting for transfers between devices: 49.8 us -> 4.22 us  [local(): lax.all_to_all(moe_col, 'grp', split_axis=0, concat_axis=1, tiled=True)]
    reshape x4 -> x0, local copies, waits for them, and re-layouts: 22.9 us -> none  [the longest x1 6.8 us: local(): expert_out.reshape(ep_devices, capacity * SLOTS_DEV, width_part)]
    all_gather x0 -> x2, waiting for transfers between devices: none -> 18.4 us  [the longest x1 18.4 us: local(): rows_all = lax.all_gather(normed, 'ep', axis=0)]
    scatter x1 -> x0, local copies, waits for them, and re-layouts: 7.38 us -> none  [local(): outgoing = jnp.zeros((ep_devices * capacity * SLOTS_DEV, width_part), jnp...]
  transfers between devices with their start and end apart: 4 -> 7, of which waited for: 3 -> 5; matrix products, arithmetic and copies ran while one was open for 3% -> 4% of each run, Pallas kernels for 0% -> 0%
where the time goes in v1:
time: 435 us; the launch traced here: 433 us
  waiting for transfers between devices  225 us (52%)
  blocking collectives  139 us (32%)
  matrix products  24.9 us (6%)
  between operations  14 us (3%)
  other arithmetic  12.9 us (3%)
  starting transfers between devices  11.9 us (3%)
  local copies, waits for them, and re-layouts  6.18 us (1%)
    reduce_scatter x1, waiting for transfers between devices, local(): mixture = lax.psum_scatter(mixture, 'ep', scatter_dimension=0, tiled=False)  146 us
    reduce_scatter x1, waiting for transfers between devices, local(): lax.psum_scatter(partial_term, 'grp', scatter_dimension=1, tiled=True)  51.1 us
    all_gather x1, blocking collectives, local(): ids_all = lax.all_gather(ids_col, 'ep', axis=0)  46.6 us
    all_gather x1, blocking collectives, local(): share_all = lax.all_gather(route_share, 'ep', axis=0)  44.4 us
    all_gather x1, waiting for transfers between devices, local(): rows_all = lax.all_gather(normed, 'ep', axis=0)  18.4 us
    all_gather x1, blocking collectives, local(): lax.all_gather(context, 'grp', axis=0, tiled=True)  14.5 us
    all_gather x1, blocking collectives, local(): lax.all_gather(expert_ids, 'grp', axis=0, tiled=True)  11.9 us
    psum x1, blocking collectives, local(): sum_squares = lax.psum(jnp.sum(attended_f * attended_f, axis=1), 'grp')  10.7 us
  transfers between devices with their start and end apart: 7, of which 5 were waited for; matrix products, arithmetic and copies ran while one was open for 4% of the time, Pallas kernels for 0%

profile of v1, /device:TPU:32, one launch (start us, length us, event | category | flops | bytes accessed | tf_op | source)
XLA Modules:
  0.0 433.1 jit_solution(6127606662466355972)
XLA Ops:
  7.2 1.7 copy.121
  8.9 4.3 all-to-all-start
  15.5 1.3 iota_compare_fusion.1
  20.8 1.3 fusion.55
  22.9 14.5 %all_gather.36 = bf16[96,4096]{1,0:T(8,128)(2,1)S(1)} all-gather(bf16[24,4096]{1,0:T(8,128)(2,1)S(1)} %pad_maximum_fusion), channel_id=1, replica_groups=mesh['grp'=4,'ep'=64] {'grp'}, dimensions={0}, use_global_device_ids=true | all-gather | bytes 983040 | tf_op jit(solution)/shard_map/all_gather | solution.py:113
  38.4 3.1 multiply_reduce_fusion
  41.5 10.7 %psum.7 = f32[96]{0:T(128)S(1)} all-reduce(f32[96]{0:T(128)S(1)} %get-tuple-element.12), channel_id=1, replica_groups=mesh['grp'=4,'ep'=64] {'grp'}, use_global_device_ids=true, to_apply=%region_11.12 | all-reduce | flops 96 | bytes 768 | tf_op jit(solution)/shard_map/psum | solution.py:123
  53.0 11.9 %all-gather.3 = s32[4,24,8]{1,2,0:T(8,128)S(1)} all-gather(s32[1,24,8]{1,2,0:T(8,128)S(1)} %bitcast.133), channel_id=1, replica_groups=mesh['grp'=4,'ep'=64] {'grp'}, dimensions={0}, use_global_device_ids=true | all-gather | bytes 3840 | tf_op jit(solution)/shard_map/all_gather | solution.py:114
  65.1 46.6 %all-gather.4 = s32[64,96,8]{1,2,0:T(8,128)S(1)} all-gather(s32[1,96,8]{1,2,0:T(8,128)S(1)} %reshape.156), channel_id=2, replica_groups=mesh['grp'=4,'ep'=64] {'ep'}, dimensions={0}, use_global_device_ids=true | all-gather | bytes 199680 | tf_op jit(solution)/shard_map/all_gather | solution.py:132
  115.5 18.4 %all-gather.12.cloned.1.call-done = bf16[6144,512]{1,0:T(8,128)(2,1)} async-done(((bf16[96,512]{1,0:T(8,128)(2,1)}), bf16[6144,512]{1,0:T(8,128)(2,1)}) %all-gather.12.cloned.1.call-update) | async-done | bytes 6291472 | tf_op jit(solution)/shard_map/all_gather | solution.py:134
  133.9 3.7 fusion.5
  137.6 6.6 %convolution_convert_fusion = bf16[3,512,1536]{2,1,0:T(8,128)(2,1)} fusion(bf16[3,512,1536]{2,1,0:T(8,128)(2,1)} %param.26, bf16[3,64,8,512]{3,2,0,1:T(8,128)(2,1)S(1)} %fusion.5), kind=kOutput, calls=%fused_computation.2 | convolution fusion | flops 2418278400 | bytes 11010048 | tf_op jit(solution)/shard_map/jnd,jdf->jnf/dot_general | solution.py:158
  144.3 51.1 %reduce-scatter.3.cloned.1.call-done = bf16[3,128,1536]{2,1,0:T(8,128)(2,1)} async-done(((bf16[3,512,1536]{2,1,0:T(8,128)(2,1)}), bf16[3,128,1536]{2,1,0:T(8,128)(2,1)}) %reduce-scatter.3.cloned.1.call-update) | async-done | bytes 1179664 | tf_op jit(solution)/shard_map/reduce_scatter | solution.py:161
  195.4 1.5 convert_element_type.126
  198.2 10.4 %all-gather.5 = bf16[4,24,8]{1,2,0:T(8,128)(2,1)S(1)} all-gather(bf16[1,24,8]{1,2,0:T(8,128)(2,1)S(1)} %bitcast.134), channel_id=1, replica_groups=mesh['grp'=4,'ep'=64] {'grp'}, dimensions={0}, use_global_device_ids=true | all-gather | bytes 1920 | tf_op jit(solution)/shard_map/all_gather | solution.py:115
  208.8 44.4 %all-gather.6 = f32[64,96,8]{1,2,0:T(8,128)S(1)} all-gather(f32[1,96,8]{1,2,0:T(8,128)S(1)} %divide_bitcast_fusion), channel_id=3, replica_groups=mesh['grp'=4,'ep'=64] {'ep'}, dimensions={0}, use_global_device_ids=true | all-gather | bytes 199680 | tf_op jit(solution)/shard_map/all_gather | solution.py:133
  253.6 3.0 fusion.4
  256.6 4.5 %bitcast_convert_fusion = bf16[64,96,512]{2,1,0:T(8,128)(2,1)} fusion(bf16[3,64,8,512]{3,2,1,0:T(8,128)(2,1)S(1)} %fusion.4, bf16[64,3,96]{2,1,0:T(4,128)(2,1)S(1)} %fusion.15, s32[64,3,96]{2,1,0:T(4,128)S(1)} %copy.59, pred[64,3,96]{2,1,0:T(4,128)(4,1)S(1)} %copy.58), kind=kOutput, calls=%fused_computation.1 | convolution fusion | flops 154583040 | bytes 7993344 | tf_op jit(solution)/shard_map/sjtr,jstd->srd/dot_general | solution.py:169
  261.1 145.7 %reduce-scatter.5.cloned.1.call-done = bf16[1,96,512]{2,1,0:T(8,128)(2,1)} async-done(((bf16[64,96,512]{2,1,0:T(8,128)(2,1)}), bf16[1,96,512]{2,1,0:T(8,128)(2,1)}) %reduce-scatter.5.cloned.1.call-update) | async-done | bytes 98320 | tf_op jit(solution)/shard_map/reduce_scatter | solution.py:172
  406.9 4.2 all-to-all-start.1
  411.1 1.6 fusion.29
  412.7 4.2 all-to-all-done.1
  416.9 3.3 all-to-all-start.2
  420.8 5.1 %all-to-all-done.2 = bf16[4,24,512]{2,1,0:T(8,128)(2,1)S(1)} async-done(((bf16[4,24,512]{2,1,0:T(8,128)(2,1)}), bf16[4,24,512]{2,1,0:T(8,128)(2,1)S(1)}, u32[]{:S(2)}, u32[]{:S(2)}) %all-to-all-start.2) | async-done | bytes 98336 | tf_op jit(solution)/shard_map/all_to_all | solution.py:178
  (69 shorter events, 15.8 us)
Async XLA Ops:
  7.2 246.4 %copy-start = (bf16[3,768,512]{2,1,0:T(8,128)(2,1)S(1)}, bf16[3,768,512]{2,1,0:T(8,128)(2,1)}, u32[]{:S(2)}) copy-start(bf16[3,768,512]{2,1,0:T(8,128)(2,1)} %param.27) | copy-start | bytes 7077892
  7.2 13.6 %copy-start.1 = (bf16[16,48,512]{2,1,0:T(8,128)(2,1)S(1)}, bf16[16,48,512]{2,1,0:T(8,128)(2,1)}, u32[]{:S(2)}) copy-start(bf16[16,48,512]{2,1,0:T(8,128)(2,1)} %param.17) | copy-start | bytes 2359300
  8.9 28.5 %all-to-all-start = ((bf16[24,4,512]{2,0,1:T(8,128)(2,1)}), bf16[24,4,512]{2,0,1:T(8,128)(2,1)}, u32[]{:S(2)}, u32[]{:S(2)}) async-start(bf16[24,4,512]{2,0,1:T(8,128)(2,1)} %bitcast.118), calls=%async_computation | async-start | bytes 196608 | tf_op jit(solution)/shard_map/all_to_all | solution.py:117
  13.2 120.7 %all-gather.12.cloned.1.call-start = ((), (), s32[]{:S(2)}) async-start(), calls=%async_computation.8 | async-start | bytes 6389760 | tf_op jit(solution)/shard_map/all_gather | solution.py:134
  19.6 2.8 copy-start.6
  38.3 13.9 %copy-start.3 = (f32[512]{0:T(512)S(1)}, f32[512]{0:T(512)}, u32[]{:S(2)}) copy-start(f32[512]{0:T(512)} %param.22) | copy-start | bytes 6148
  38.3 14.7 %copy-start.2 = (s32[24,8]{0,1:T(8,128)S(1)}, s32[24,8]{0,1:T(8,128)}, u32[]{:S(2)}) copy-start(s32[24,8]{0,1:T(8,128)} %param.23) | copy-start | bytes 2308
  38.3 26.7 %copy-start.5 = (s32[192]{0:T(256)S(1)}, s32[192]{0:T(256)}, u32[]{:S(2)}) copy-start(s32[192]{0:T(256)} %param.25) | copy-start | bytes 2308
  53.0 142.4 %reduce-scatter.3.cloned.1.call-start = ((), (), s32[]{:S(2)}) async-start(), calls=%async_computation.5 | async-start | bytes 5898240 | tf_op jit(solution)/shard_map/reduce_scatter | solution.py:161
  144.2 109.3 %all-gather.10.cloned.1.call-start = ((), (), s32[]{:S(2)}) async-start(), calls=%async_computation.6 | async-start | bytes 2949120 | tf_op jit(solution)/shard_map/all_gather | solution.py:163
  196.9 1.3 copy-start.4
  198.1 208.7 %reduce-scatter.5.cloned.1.call-start = ((), (), s32[]{:S(2)}) async-start(), calls=%async_computation.7 | async-start | bytes 6389760 | tf_op jit(solution)/shard_map/reduce_scatter | solution.py:172
  406.9 10.0 %all-to-all-start.1 = ((bf16[4,24,512]{2,1,0:T(8,128)(2,1)}), bf16[4,24,512]{2,1,0:T(8,128)(2,1)S(1)}, u32[]{:S(2)}, u32[]{:S(2)}) async-start(bf16[4,24,512]{2,1,0:T(8,128)(2,1)} %bitcast.125), calls=%async_computation.3 | async-start | bytes 196608 | tf_op jit(solution)/shard_map/all_to_all | solution.py:177
  416.9 9.1 %all-to-all-start.2 = ((bf16[4,24,512]{2,1,0:T(8,128)(2,1)}), bf16[4,24,512]{2,1,0:T(8,128)(2,1)S(1)}, u32[]{:S(2)}, u32[]{:S(2)}) async-start(bf16[4,24,512]{2,1,0:T(8,128)(2,1)} %bitcast.27), calls=%async_computation.4 | async-start | bytes 196608 | tf_op jit(solution)/shard_map/all_to_all | solution.py:178
Sparse Core Ops, SparseCore 0:
  53.1 80.7 all-gather.11
  144.3 50.9 reduce-scatter.2
  198.3 35.2 all-gather.9
  261.2 145.5 reduce-scatter.4

commit v2 on v1

v2 whole, which is shorter than its diff:
```python
import functools
import math

import jax
import jax.numpy as jnp
from jax import lax
from jax.experimental import pallas as pl
from jax.experimental.pallas import tpu as pltpu
from jax.sharding import PartitionSpec as P

D = 2048
HEADS = 32
KV_HEADS = 4
HEAD_DIM = 128
FF = 768
TOPK = 8
SLOTS_DEV = 3
PRE = 8
DEV_ROWS = 24
COL_ROWS = 96
DQ = 512
HALF = 256
NX = 4
NY = 4
NZ = 8
SPAN = 8

MESH = pl.DeviceIdType.MESH
F32 = jnp.float32
BF16 = jnp.bfloat16

masked_score = -1e30
epsilon = 1e-06


def prefill_context(queries, new_keys, new_values):
    head_group = HEADS // KV_HEADS
    scaling = 1.0 / math.sqrt(HEAD_DIM)
    query_pre = queries[:PRE].reshape(PRE, KV_HEADS, head_group, HEAD_DIM)
    keys_pre = new_keys[:PRE].reshape(PRE, KV_HEADS, HEAD_DIM)
    values_pre = new_values[:PRE].reshape(PRE, KV_HEADS, HEAD_DIM)
    scores = (
        jnp.einsum("ikgd,jkd->kgij", query_pre, keys_pre, preferred_element_type=jnp.float32)
        * scaling
    )
    causal = jnp.arange(PRE)[:, None] >= jnp.arange(PRE)[None, :]
    scores = jnp.where(causal, scores, masked_score)
    exponent = jnp.exp(scores - jnp.max(scores, axis=-1, keepdims=True))
    attn_probs = (exponent / jnp.sum(exponent, axis=-1, keepdims=True)).astype(jnp.bfloat16)
    mixed_values = jnp.einsum(
        "kgij,jkd->ikgd", attn_probs, values_pre, preferred_element_type=jnp.float32
    )
    return mixed_values.astype(jnp.bfloat16).reshape(PRE, HEADS * HEAD_DIM)


def decode_context(queries, new_keys, new_values, key_cache, value_cache, cache_len):
    requests = key_cache.shape[0]
    cache_slots = key_cache.shape[1]
    head_group = HEADS // KV_HEADS
    scaling = 1.0 / math.sqrt(HEAD_DIM)
    query_dec = queries[PRE:].reshape(requests, KV_HEADS, head_group, HEAD_DIM)
    keys_dec = new_keys[PRE:].reshape(requests, KV_HEADS, HEAD_DIM)
    values_dec = new_values[PRE:].reshape(requests, KV_HEADS, HEAD_DIM)
    cached_keys = key_cache.reshape(requests, cache_slots, KV_HEADS, HEAD_DIM)
    cached_values = value_cache.reshape(requests, cache_slots, KV_HEADS, HEAD_DIM)
    cache_scores = (
        jnp.einsum("nkgd,ntkd->nkgt", query_dec, cached_keys, preferred_element_type=jnp.float32)
        * scaling
    )
    own_score = (
        jnp.einsum("nkgd,nkd->nkg", query_dec, keys_dec, preferred_element_type=jnp.float32)
        * scaling
    )
    valid = jnp.arange(cache_slots)[None, :] < cache_len[:, None]
    cache_scores = jnp.where(valid[:, None, None, :], cache_scores, masked_score)
    top_score = jnp.maximum(jnp.max(cache_scores, axis=-1), own_score)
    cache_exp = jnp.exp(cache_scores - top_score[..., None])
    own_exp = jnp.exp(own_score - top_score)
    denominator = jnp.sum(cache_exp, axis=-1) + own_exp
    cache_probs = (cache_exp / denominator[..., None]).astype(jnp.bfloat16)
    own_probs = (own_exp / denominator).astype(jnp.bfloat16)
    mixed_values = jnp.einsum(
        "nkgt,ntkd->nkgd", cache_probs, cached_values, preferred_element_type=jnp.float32
    )
    mixed_values = (
        mixed_values
        + own_probs.astype(jnp.float32)[..., None] * values_dec.astype(jnp.float32)[:, :, None, :]
    )
    return mixed_values.astype(jnp.bfloat16).reshape(requests, HEADS * HEAD_DIM)


CTX_R, CTX_L, CTX_FR, CTX_FL = 0, 1, 2, 3
SIDE = 4
SQUARES = 7
A_RING_R, A_RING_L = 10, 14
B_Y = 17
B_RING_R, B_RING_L = 21, 25
A_Y = 28
A_RELAY = 44
CORE_A = 60
CORE_B = 64
S1_R, S1_L, S2_R, S2_L = 72, 80, 88, 96
H1_R, H1_L, H2_R, H2_L = 104, 112, 120, 128
CORE_MIX = 136
CHAIN = 144
Y_ONE = 152
Y_TWO = 154
FINAL = 156
COPIES = 160


def layer_kernel(
    ctx_ref,
    side_ref,
    out_proj_hbm,
    gain_ref,
    table_ref,
    gate_up_hbm,
    down_hbm,
    moe_ref,
    layer_ref,
    ctx_all,
    side_all,
    proj,
    gate_up,
    down,
    squares,
    attended,
    rows_a,
    rows_b,
    picks,
    picked,
    partial,
    first_in,
    second_in,
    hidden,
    expert_out,
    mixed,
    core_in,
    chain_out,
    chain_in,
    y_part,
    y_one,
    y_two,
    final_out,
    final_in,
    send_sem,
    recv_sem,
    load_sem,
):
    x = lax.axis_index("grp")
    ep = lax.axis_index("ep")
    core = ep % 2
    z = (ep // 2) % NZ
    y = ep // (2 * NZ)

    def x_dev(step):
        return ((x + step) % NX, ep)

    def y_dev(step):
        return (x, (((y + step) % NY) * NZ + z) * 2 + core)

    def z_dev(step):
        return (x, (y * NZ + (z + step) % NZ) * 2 + core)

    partner = (x, (y * NZ + z) * 2 + 1 - core)

    def copy(source, target, index, device):
        return pltpu.make_async_remote_copy(
            src_ref=source,
            dst_ref=target,
            send_sem=send_sem.at[index],
            recv_sem=recv_sem.at[index],
            device_id=device,
            device_id_type=MESH,
        )

    peers = [x_dev(1), x_dev(2), x_dev(3), y_dev(1), y_dev(3), z_dev(1), z_dev(7), partner]
    barrier = pltpu.get_barrier_semaphore()
    for peer in peers:
        pl.semaphore_signal(barrier, inc=1, device_id=peer, device_id_type=MESH)

    loads = [
        pltpu.make_async_copy(out_proj_hbm, proj, load_sem.at[0]),
        pltpu.make_async_copy(gate_up_hbm, gate_up, load_sem.at[1]),
        pltpu.make_async_copy(down_hbm, down, load_sem.at[2]),
        pltpu.make_async_copy(ctx_ref, ctx_all.at[x], load_sem.at[3]),
        pltpu.make_async_copy(side_ref.at[x], side_all.at[x], load_sem.at[4]),
    ]
    for load in loads:
        load.start()
    pl.semaphore_wait(barrier, len(peers))

    pending = []

    def send(source, target, index, device):
        made = copy(source, target, index, device)
        made.start()
        pending.append(made)
        return made

    ctx_r = send(ctx_ref, ctx_all.at[x], CTX_R, x_dev(1))
    ctx_l = send(ctx_ref, ctx_all.at[x], CTX_L, x_dev(3))
    sides = []
    for step in (1, 2, 3):
        there = (x + step) % NX
        sides.append(send(side_ref.at[there], side_all.at[x], SIDE + step - 1, x_dev(step)))
    from_l, from_r = (x + 3) % NX, (x + 1) % NX
    ctx_r.wait_recv()
    low, high = pl.ds(0, D // 2), pl.ds(D // 2, D // 2)
    fwd_r = send(
        ctx_all.at[from_l, :, low], ctx_all.at[from_l, :, low], CTX_FR, x_dev(1)
    )
    ctx_l.wait_recv()
    fwd_l = send(
        ctx_all.at[from_r, :, high], ctx_all.at[from_r, :, high], CTX_FL, x_dev(3)
    )
    loads[0].wait()
    loads[3].wait()
    loads[4].wait()
    for side in sides:
        side.wait_recv()
    fwd_r.wait_recv()
    fwd_l.wait_recv()

    context = ctx_all[...].reshape(NX * 2 * DEV_ROWS, D)
    first = jnp.dot(context, proj[0:D, :], preferred_element_type=F32)
    second = jnp.dot(context, proj[D : 2 * D, :], preferred_element_type=F32)
    for g in range(NX):
        base = g * 2 * DEV_ROWS
        block = first[base : base + DEV_ROWS] + second[base + DEV_ROWS : base + 2 * DEV_ROWS]
        residual = side_all[g, 0:32, :].astype(F32)[0:DEV_ROWS]
        attended[g * DEV_ROWS : (g + 1) * DEV_ROWS, :] = (
            (residual + block).astype(BF16).astype(F32)
        )
    att = attended[...]
    total = jnp.sum(att * att, axis=1, keepdims=True)
    squares[x] = jnp.broadcast_to(total, (COL_ROWS, 128))
    shares = [
        send(squares.at[x], squares.at[x], SQUARES + step - 1, x_dev(step)) for step in (1, 2, 3)
    ]
    meta = (
        side_all[0, 32:48, 0:HALF].astype(F32)
        + side_all[1, 32:48, 0:HALF].astype(F32)
        + side_all[2, 32:48, 0:HALF].astype(F32)
        + side_all[3, 32:48, 0:HALF].astype(F32)
    )
    rows_a[core, y, z, COL_ROWS : COL_ROWS + 16, :] = meta.astype(BF16)
    for share in shares:
        share.wait_recv()
    total = squares[0][:, 0:1] + squares[1][:, 0:1] + squares[2][:, 0:1] + squares[3][:, 0:1]
    normed = (att * lax.rsqrt(total / D + epsilon) * gain_ref[...]).astype(BF16)
    rows_a[core, y, z, 0:COL_ROWS, :] = normed[:, 0:HALF]
    rows_b[core, z, y] = normed[:, HALF:DQ]

    def own_a(where):
        return rows_a.at[core, y, where]

    b_right = send(rows_b.at[core, z, y], rows_b.at[core, z, y], B_Y, y_dev(1))
    b_left = send(rows_b.at[core, z, y], rows_b.at[core, z, y], B_Y + 1, y_dev(3))
    a_right = [send(own_a(z), own_a(z), A_RING_R, z_dev(1))]
    a_left = [send(own_a(z), own_a(z), A_RING_L, z_dev(7))]
    a_over = []

    def a_out(where, number):
        a_over.append(send(own_a(where), own_a(where), A_Y + 2 * number, y_dev(1)))
        a_over.append(send(own_a(where), own_a(where), A_Y + 2 * number + 1, y_dev(3)))

    a_out(z, 0)
    y_l, y_r = (y + 3) % NY, (y + 1) % NY
    top, bottom = pl.ds(0, 48), pl.ds(48, 48)
    b_right.wait_recv()
    b_fr = send(rows_b.at[core, z, y_l, top], rows_b.at[core, z, y_l, top], B_Y + 2, y_dev(1))
    b_left.wait_recv()
    b_fl = send(
        rows_b.at[core, z, y_r, bottom], rows_b.at[core, z, y_r, bottom], B_Y + 3, y_dev(3)
    )
    a_right[0].wait_recv()
    left = (z + 7) % NZ
    a_right.append(send(own_a(left), own_a(left), A_RING_R + 1, z_dev(1)))
    a_out(left, 1)
    a_left[0].wait_recv()
    right = (z + 1) % NZ
    a_left.append(send(own_a(right), own_a(right), A_RING_L + 1, z_dev(7)))
    a_out(right, 2)
    b_fr.wait_recv()
    b_fl.wait_recv()
    b_slab = rows_b.at[core, z]
    z_right = [send(b_slab, b_slab, B_RING_R, z_dev(1))]
    z_left = [send(b_slab, b_slab, B_RING_L, z_dev(7))]
    core_copies = [send(b_slab, b_slab, CORE_B, partner)]
    number = 3
    for step in (2, 3, 4):
        a_right[step - 1].wait_recv()
        left = (z + NZ - step) % NZ
        if step < 4:
            a_right.append(send(own_a(left), own_a(left), A_RING_R + step, z_dev(1)))
        a_out(left, number)
        number += 1
        if step < 4:
            a_left[step - 1].wait_recv()
            right = (z + step) % NZ
            if step < 3:
                a_left.append(send(own_a(right), own_a(right), A_RING_L + step, z_dev(7)))
            a_out(right, number)
            number += 1
    core_copies.append(send(rows_a.at[core, y], rows_a.at[core, y], CORE_A, partner))

    def a_relay(number, where):
        a_over[2 * number].wait_recv()
        a_over[2 * number + 1].wait_recv()
        if number % 2 == 0:
            block = rows_a.at[core, y_l, where]
            return send(block, block, A_RELAY + number, y_dev(1))
        block = rows_a.at[core, y_r, where]
        return send(block, block, A_RELAY + number, y_dev(3))

    order = [z, (z + 7) % NZ, (z + 1) % NZ, (z + 6) % NZ, (z + 2) % NZ, (z + 5) % NZ]
    order += [(z + 3) % NZ, (z + 4) % NZ]
    relays = []
    for step in (1, 2, 3, 4):
        z_right[step - 1].wait_recv()
        slab = rows_b.at[core, (z + NZ - step) % NZ]
        if step < 4:
            z_right.append(send(slab, slab, B_RING_R + step, z_dev(1)))
        core_copies.append(send(slab, slab, CORE_B + 2 * step - 1, partner))
        for number in (2 * step - 2, 2 * step - 1):
            relays.append(a_relay(number, order[number]))
        if step < 4:
            z_left[step - 1].wait_recv()
            slab = rows_b.at[core, (z + step) % NZ]
            if step < 3:
                z_left.append(send(slab, slab, B_RING_L + step, z_dev(7)))
            core_copies.append(send(slab, slab, CORE_B + 2 * step, partner))
    for there, number in ((y_l, 1), (y_r, 2)):
        slab = rows_a.at[core, there]
        core_copies.append(send(slab, slab, CORE_A + number, partner))
    for relay in relays:
        relay.wait_recv()
    slab = rows_a.at[core, (y + 2) % NY]
    core_copies.append(send(slab, slab, CORE_A + 3, partner))
    for made in core_copies:
        made.wait_recv()
    loads[1].wait()
    loads[2].wait()

    opposite = (x + 2) % NX
    lower, upper = pl.ds(0, FF), pl.ds(FF, FF)

    def chunk_of(k):
        odd = k % 2
        return (z + NZ + (1 - odd) * (4 - k // 2) + odd * (k // 2 - 3)) % NZ

    def first_copies(k):
        return (
            copy(partial.at[k, opposite, :, lower], first_in.at[k, 0], S1_R + k, x_dev(1)),
            copy(partial.at[k, opposite, :, upper], first_in.at[k, 1], S1_L + k, x_dev(3)),
        )

    def second_copies(k):
        return (
            copy(partial.at[k, from_r], second_in.at[k, 0], S2_R + k, x_dev(1)),
            copy(partial.at[k, from_l], second_in.at[k, 1], S2_L + k, x_dev(3)),
        )

    def hidden_copies(k):
        return (
            copy(hidden.at[k, x], hidden.at[k, x], H1_R + k, x_dev(1)),
            copy(hidden.at[k, x], hidden.at[k, x], H1_L + k, x_dev(3)),
        )

    near, far = pl.ds(0, FF // 2), pl.ds(FF // 2, FF // 2)

    def forward_copies(k):
        return (
            copy(hidden.at[k, from_l, :, near], hidden.at[k, from_l, :, near], H2_R + k, x_dev(1)),
            copy(hidden.at[k, from_r, :, far], hidden.at[k, from_r, :, far], H2_L + k, x_dev(3)),
        )

    def core_copy(k):
        return copy(mixed.at[k, 1 - core], core_in.at[k], CORE_MIX + k, partner)

    def chain_right(k):
        return copy(chain_out.at[k], chain_in.at[k], CHAIN + k, z_dev(1))

    def chain_left(k):
        return copy(chain_out.at[k], chain_in.at[k], CHAIN + k, z_dev(7))

    row_iota = lax.broadcasted_iota(jnp.int32, (COL_ROWS, COL_ROWS), 0)
    lane_iota = lax.broadcasted_iota(jnp.int32, (COL_ROWS, COL_ROWS), 1)
    earlier = (row_iota < lane_iota).astype(F32).astype(BF16)
    place = lax.broadcasted_iota(jnp.int32, (SPAN, COL_ROWS), 0).astype(F32)

    def pick_and_multiply(k):
        g = chunk_of(k)
        for column in range(2 * NY):
            cy, cc = column // 2, column % 2
            meta = rows_a[cc, cy, g, COL_ROWS : COL_ROWS + 16, :].astype(F32)[:, 0:COL_ROWS]
            ids, weights = meta[0:TOPK], meta[TOPK : 2 * TOPK]
            scale = 1.0 / jnp.sum(weights, axis=0, keepdims=True)
            named, share = [], []
            for j in range(SLOTS_DEV):
                same = (ids == table_ref[j : j + 1, 0:COL_ROWS]).astype(F32)
                named.append(jnp.sum(same, axis=0, keepdims=True))
                share.append(jnp.sum(same * weights, axis=0, keepdims=True) * scale)
            padded = jnp.concatenate(
                named + [jnp.zeros((SPAN - SLOTS_DEV, COL_ROWS), F32)], axis=0
            )
            ranks = jnp.dot(padded.astype(BF16), earlier, preferred_element_type=F32)
            chosen, weighted = [], []
            for j in range(SLOTS_DEV):
                rank = ranks[j : j + 1]
                twice = table_ref[3 + j : 4 + j, 0:COL_ROWS]
                parity = table_ref[6 + j : 7 + j, 0:COL_ROWS]
                halved = jnp.floor(rank * 0.5)
                where = jnp.where(twice > 0.5, halved, rank)
                odd = rank - 2.0 * halved
                good = (named[j] > 0.5) & ((twice < 0.5) | (odd == parity))
                key = jnp.where(good, where, -1.0)
                pick = (jnp.broadcast_to(key, (SPAN, COL_ROWS)) == place).astype(F32)
                chosen.append(pick)
                weighted.append(pick * share[j])
            pick = jnp.concatenate(chosen, axis=0).astype(BF16)
            picks[k % 8, column] = jnp.concatenate(weighted, axis=0)
            got_a = jnp.dot(pick, rows_a[cc, cy, g, 0:COL_ROWS, :], preferred_element_type=F32)
            got_b = jnp.dot(pick, rows_b[cc, g, cy], preferred_element_type=F32)
            for j in range(SLOTS_DEV):
                span = slice(j * SPAN, (j + 1) * SPAN)
                picked[j, column * SPAN : (column + 1) * SPAN, 0:HALF] = got_a[span]
                picked[j, column * SPAN : (column + 1) * SPAN, HALF:DQ] = got_b[span]
        for j in range(SLOTS_DEV):
            inputs = picked[j].astype(BF16)
            for part in range(3):
                lanes = slice(part * DQ, (part + 1) * DQ)
                product = jnp.dot(inputs, gate_up[j, :, lanes], preferred_element_type=F32)
                product = product.astype(BF16)
                for o in range(NX):
                    partial[k, o, j * 16 : (j + 1) * 16, lanes] = product[o * 16 : (o + 1) * 16]
        for made in first_copies(k):
            made.start()

    def add_first(k):
        for made in first_copies(k):
            made.wait_recv()
        partial[k, from_r, :, 0:FF] = (
            partial[k, from_r, :, 0:FF].astype(F32) + first_in[k, 0].astype(F32)
        ).astype(BF16)
        partial[k, from_l, :, FF : 2 * FF] = (
            partial[k, from_l, :, FF : 2 * FF].astype(F32) + first_in[k, 1].astype(F32)
        ).astype(BF16)
        for made in second_copies(k):
            made.start()

    def add_second(k):
        for made in second_copies(k):
            made.wait_recv()
        summed = (
            partial[k, x].astype(F32) + second_in[k, 0].astype(F32) + second_in[k, 1].astype(F32)
        )
        gate, up = summed[:, 0:FF], summed[:, FF : 2 * FF]
        hidden[k, x] = (gate / (1.0 + jnp.exp(-gate)) * up).astype(BF16)
        for made in hidden_copies(k):
            made.start()

    def pass_hidden(k):
        for made in hidden_copies(k):
            made.wait_recv()
        for made in forward_copies(k):
            made.start()

    def mix(k):
        for made in forward_copies(k):
            made.wait_recv()
        for j in range(SLOTS_DEV):
            inputs = hidden[k, :, j * 16 : (j + 1) * 16, :].reshape(NX * 16, FF)
            product = jnp.dot(inputs, down[j], preferred_element_type=F32)
            expert_out[j] = product.astype(BF16).astype(F32)
        for column in range(2 * NY):
            cy, cc = column // 2, column % 2
            span = slice(column * SPAN, (column + 1) * SPAN)
            results = jnp.concatenate([expert_out[j, span] for j in range(SLOTS_DEV)], axis=0)
            mixture = lax.dot_general(
                picks[k % 8, column].astype(BF16),
                results.astype(BF16),
                (((0,), (0,)), ((), ())),
                preferred_element_type=F32,
            )
            mixed[k, cc, cy] = mixture.astype(BF16)
        core_copy(k).start()

    def chain(k):
        core_copy(k).wait_recv()

        @pl.when(k < 2)
        def _():
            chain_out[k] = (mixed[k, core].astype(F32) + core_in[k].astype(F32)).astype(BF16)

        @pl.when((k >= 2) & (k < NZ - 1))
        def _():
            chain_right(k - 2).wait_recv()
            chain_out[k] = (
                mixed[k, core].astype(F32) + core_in[k].astype(F32) + chain_in[k - 2].astype(F32)
            ).astype(BF16)

        @pl.when((k < NZ - 1) & (k % 2 == 0))
        def _():
            chain_right(k).start()

        @pl.when((k < NZ - 1) & (k % 2 == 1))
        def _():
            chain_left(k).start()

    def tick(t, carry):
        for stage, work in ((5, chain), (4, mix), (3, pass_hidden), (2, add_second), (1, add_first)):
            pl.when((t >= stage) & (t < NZ + stage))(functools.partial(work, t - stage))
        pl.when(t < NZ)(functools.partial(pick_and_multiply, t))
        return carry

    lax.fori_loop(0, NZ + 6, tick, 0)

    last = NZ - 1
    chain_right(last - 2).wait_recv()
    chain_right(last - 1).wait_recv()
    for there in range(NY):
        y_part[there] = (
            mixed[last, core, there].astype(F32)
            + core_in[last, there].astype(F32)
            + chain_in[last - 2, there].astype(F32)
            + chain_in[last - 1, there].astype(F32)
        ).astype(BF16)
    y_far = (y + 2) % NY
    one_r = send(y_part.at[y_far, top], y_one.at[0], Y_ONE, y_dev(1))
    one_l = send(y_part.at[y_far, bottom], y_one.at[1], Y_ONE + 1, y_dev(3))
    one_r.wait_recv()
    y_part[y_r, 0:48, :] = (
        y_part[y_r, 0:48, :].astype(F32) + y_one[0].astype(F32)
    ).astype(BF16)
    two_r = send(y_part.at[y_r], y_two.at[0], Y_TWO, y_dev(1))
    one_l.wait_recv()
    y_part[y_l, 48:96, :] = (
        y_part[y_l, 48:96, :].astype(F32) + y_one[1].astype(F32)
    ).astype(BF16)
    two_l = send(y_part.at[y_l], y_two.at[1], Y_TWO + 1, y_dev(3))
    two_r.wait_recv()
    two_l.wait_recv()
    mixture = y_part[y].astype(F32) + y_two[0].astype(F32) + y_two[1].astype(F32)
    both = attended[...] + mixture
    for g in range(NX):
        span = slice(g * DEV_ROWS, (g + 1) * DEV_ROWS)
        final_out[g] = jnp.concatenate([mixture[span], both[span]], axis=0).astype(BF16)
    finals = []
    for step in (1, 2, 3):
        there = (x + step) % NX
        finals.append(send(final_out.at[there], final_in.at[x], FINAL + step - 1, x_dev(step)))
    final_in[x] = final_out[x]
    for made in finals:
        made.wait_recv()
    for g in range(NX):
        block = final_in[g].astype(F32)
        lanes = slice(g * DQ, (g + 1) * DQ)
        moe_ref[:, lanes] = block[0:DEV_ROWS].astype(BF16)
        layer_ref[:, lanes] = block[DEV_ROWS : 2 * DEV_ROWS].astype(BF16)

    def drain(k, carry):
        for made in (
            *first_copies(k),
            *second_copies(k),
            *hidden_copies(k),
            *forward_copies(k),
            core_copy(k),
        ):
            made.wait_send()

        @pl.when(k < NZ - 1)
        def _():
            chain_right(k).wait_send()

        return carry

    lax.fori_loop(0, NZ, drain, 0)
    for made in pending:
        made.wait_send()


def whole_layer(ctx, side, out_proj, gain, table, gate_up, down_proj):
    vmem = pl.BlockSpec(memory_space=pltpu.VMEM)
    hbm = pl.BlockSpec(memory_space=pl.ANY)
    return pl.pallas_call(
        layer_kernel,
        out_shape=(
            jax.ShapeDtypeStruct((DEV_ROWS, D), BF16),
            jax.ShapeDtypeStruct((DEV_ROWS, D), BF16),
        ),
        in_specs=[vmem, vmem, hbm, vmem, vmem, hbm, hbm],
        out_specs=(vmem, vmem),
        scratch_shapes=[
            pltpu.VMEM((NX, 2 * DEV_ROWS, D), BF16),
            pltpu.VMEM((NX, 48, DQ), BF16),
            pltpu.VMEM((2 * D, DQ), BF16),
            pltpu.VMEM((SLOTS_DEV, DQ, 2 * FF), BF16),
            pltpu.VMEM((SLOTS_DEV, FF, DQ), BF16),
            pltpu.VMEM((NX, COL_ROWS, 128), F32),
            pltpu.VMEM((COL_ROWS, DQ), F32),
            pltpu.VMEM((2, NY, NZ, COL_ROWS + 16, HALF), BF16),
            pltpu.VMEM((2, NZ, NY, COL_ROWS, HALF), BF16),
            pltpu.VMEM((NZ, 2 * NY, SLOTS_DEV * SPAN, COL_ROWS), F32),
            pltpu.VMEM((SLOTS_DEV, 2 * NY * SPAN, DQ), F32),
            pltpu.VMEM((NZ, NX, 48, 2 * FF), BF16),
            pltpu.VMEM((NZ, 2, 48, FF), BF16),
            pltpu.VMEM((NZ, 2, 48, 2 * FF), BF16),
            pltpu.VMEM((NZ, NX, 48, FF), BF16),
            pltpu.VMEM((SLOTS_DEV, 2 * NY * SPAN, DQ), F32),
            pltpu.VMEM((NZ, 2, NY, COL_ROWS, DQ), BF16),
            pltpu.VMEM((NZ, NY, COL_ROWS, DQ), BF16),
            pltpu.VMEM((NZ, NY, COL_ROWS, DQ), BF16),
            pltpu.VMEM((NZ, NY, COL_ROWS, DQ), BF16),
            pltpu.VMEM((NY, COL_ROWS, DQ), BF16),
            pltpu.VMEM((2, COL_ROWS // 2, DQ), BF16),
            pltpu.VMEM((2, COL_ROWS, DQ), BF16),
            pltpu.VMEM((NX, 48, DQ), BF16),
            pltpu.VMEM((NX, 48, DQ), BF16),
            pltpu.SemaphoreType.DMA((COPIES,)),
            pltpu.SemaphoreType.DMA((COPIES,)),
            pltpu.SemaphoreType.DMA((5,)),
        ],
        compiler_params=pltpu.CompilerParams(
            collective_id=0, has_side_effects=True, vmem_limit_bytes=67043328
        ),
    )(ctx, side, out_proj, gain, table, gate_up, down_proj)


def local(
    queries,
    new_keys,
    new_values,
    key_cache,
    value_cache,
    cache_len,
    residual,
    out_proj,
    norm_gain,
    expert_ids,
    route_weights,
    slot_expert,
    gate_up,
    down_proj,
):
    x = lax.axis_index("grp")
    ep = lax.axis_index("ep")
    context = jnp.concatenate(
        [
            prefill_context(queries, new_keys, new_values),
            decode_context(queries, new_keys, new_values, key_cache, value_cache, cache_len),
        ],
        axis=0,
    )
    ctx = jnp.concatenate([context[:, :D], context[:, D:]], axis=0)
    lane = jnp.arange(HALF)[None, :] - x * DEV_ROWS
    spread = (lane == jnp.arange(DEV_ROWS)[:, None]).astype(BF16)
    both = jnp.concatenate([(expert_ids + 1).astype(BF16), route_weights], axis=1)
    meta = lax.dot_general(
        both, spread, (((0,), (0,)), ((), ())), preferred_element_type=F32
    ).astype(BF16)
    quarters = residual.reshape(DEV_ROWS, NX, DQ).transpose(1, 0, 2)
    quarters = jnp.pad(quarters, ((0, 0), (0, 8), (0, 0)))
    meta = jnp.broadcast_to(jnp.pad(meta, ((0, 0), (0, DQ - HALF)))[None], (NX, 16, DQ))
    side = jnp.concatenate([quarters, meta], axis=1)
    place = ep * SLOTS_DEV + jnp.arange(SLOTS_DEV)
    mine = lax.dynamic_slice_in_dim(slot_expert, ep * SLOTS_DEV, SLOTS_DEV)
    same = slot_expert[None, :] == mine[:, None]
    twice = jnp.sum(same, axis=1) > 1
    earlier = jnp.sum(same & (jnp.arange(slot_expert.shape[0])[None, :] < place[:, None]), axis=1)
    table = jnp.concatenate([mine + 1, twice.astype(jnp.int32), earlier, jnp.zeros((7,), jnp.int32)])
    table = jnp.broadcast_to(table.astype(F32)[:, None], (16, 128))
    return whole_layer(ctx, side, out_proj, norm_gain[None, :], table, gate_up, down_proj)


def solution(mesh):
    placed = (
        P(("grp", "ep"), None),
        P(("grp", "ep"), None),
        P(("grp", "ep"), None),
        P(("grp", "ep"), None, None),
        P(("grp", "ep"), None, None),
        P(("grp", "ep")),
        P(("grp", "ep"), None),
        P(None, "grp"),
        P("grp"),
        P(("grp", "ep"), None),
        P(("grp", "ep"), None),
        P(),
        P("ep", "grp", None),
        P("ep", None, "grp"),
    )
    return jax.shard_map(
        local,
        mesh=mesh,
        in_specs=placed,
        out_specs=(P(("grp", "ep"), None), P(("grp", "ep"), None)),
        check_vma=False,
    )
```

time: 435 us -> 177 us (0.41)
  waiting for transfers between devices: 225 us -> 0 us
  Pallas kernels: 0 us -> 158 us
  blocking collectives: 139 us -> 0 us
  matrix products: 24.9 us -> 5.54 us
  between operations: 14 us -> 0.78 us
  starting transfers between devices: 11.9 us -> 0 us
  other arithmetic: 12.9 us -> 5.01 us
    reduce_scatter x2 -> x0, waiting for transfers between devices: 197 us -> none  [the longest x1 146 us: local(): mixture = lax.psum_scatter(mixture, 'ep', scatter_dimension=0, tiled=False)]
    pallas_call x0 -> x1, Pallas kernels: none -> 158 us  [whole_layer(): pl.pallas_call(layer_kernel, out_shape=(jax.ShapeDtypeStruct((DEV_ROWS, D...]
    all_gather x5 -> x0, blocking collectives: 128 us -> none  [the longest x1 46.6 us: local(): ids_all = lax.all_gather(ids_col, 'ep', axis=0)]
    dot_general x5 -> x1, matrix products: 21 us -> 0.13 us  [local(): lax.dot_general(both, spread, (((0,), (0,)), ((), ())), preferred_element...]
    all_gather x2 -> x0, waiting for transfers between devices: 18.4 us -> none  [the longest x1 18.4 us: local(): rows_all = lax.all_gather(normed, 'ep', axis=0)]
    all_to_all x3 -> x0, starting transfers between devices: 11.8 us -> none  [the longest x1 4.29 us: local(): lax.all_to_all(residual, 'grp', split_axis=1, concat_axis=0, tiled=True)]
    psum x1 -> x0, blocking collectives: 10.7 us -> none  [local(): sum_squares = lax.psum(jnp.sum(attended_f * attended_f, axis=1), 'grp')]
    all_to_all x3 -> x0, waiting for transfers between devices: 9.34 us -> none  [the longest x1 5.12 us: local(): lax.all_to_all(layer_col, 'grp', split_axis=0, concat_axis=1, tiled=True)]
  transfers between devices with their start and end apart: 7 -> 0, of which waited for: 5 -> 0; matrix products, arithmetic and copies ran while one was open for 4% -> 0% of each run, Pallas kernels for 0% -> 0%
where the time goes in v2:
time: 177 us; the launch traced here: 176 us
  Pallas kernels  158 us (89%)
  local copies, waits for them, and re-layouts  6.5 us (4%)
  matrix products  5.54 us (3%)
  other arithmetic  5.01 us (3%)
    pallas_call x1, Pallas kernels, whole_layer(): pl.pallas_call(layer_kernel, out_shape=(jax.ShapeDtypeStruct((DEV_ROWS, D...  158 us
    unnamed x12, local copies, waits for them, and re-layouts  4.93 us

profile of v2, /device:TPU:32, one launch (start us, length us, event | category | flops | bytes accessed | tf_op | source)
XLA Modules:
  0.0 176.0 jit_solution(3096174252508979597)
XLA Ops:
  0.7 0.8 broadcast_add_fusion
  1.5 0.9 fusion.30
  2.4 0.1 add_convert_fusion.1
  2.5 0.7 broadcast_in_dim.32.table_ref
  3.1 0.9 slice_bitcast_fusion
  4.1 0.7 iota_compare_fusion.3
  4.8 1.7 fusion.42
  6.5 0.7 slice.28
  7.3 0.2 fusion.48
  7.5 0.3 fusion.12
  7.9 0.7 slice_convert_fusion
  8.6 1.5 fusion.2
  10.1 0.1 copy.63
  10.2 0.8 slice_bitcast_fusion.1
  11.0 1.1 fusion.43
  12.2 0.1 copy.25
  12.3 0.8 convolution_convert_fusion
  13.2 0.7 fusion.14.ctx_ref
  13.9 0.0 copy-done.2
  13.9 0.1 convolution_convert_fusion.1
  14.0 0.7 fusion.13.side_ref
  14.7 158.2 %shard_map.149 = (bf16[24,2048]{1,0:T(8,128)(2,1)}, bf16[24,2048]{1,0:T(8,128)(2,1)}) custom-call(bf16[48,2048]{1,0:T(8,128)(2,1)} %fusion.14.ctx_ref, bf16[4,48,512]{2,1,0:T(8,128)(2,1)} %fusion.13.side_ref, bf16[4096,512]{1,0:T(8,128)(2,1)} %out_proj_hbm.1, f32[1,512]{1,0:T(1,128)} %bitcast.91, f32[16,128]{1,0:T(8,128)} %broadcast_in_dim.32.table_ref, ...), custom_call_target="tpu_custom_call" | custom-call | tf_op jit(solution)/shard_map/pallas_call | solution.py:588
  173.0 1.5 copy.67
  174.5 1.5 copy.68
  (20 shorter events, 0.2 us)
Async XLA Ops:
  0.6 13.2 %copy-start.1 = (s32[24,8]{0,1:T(8,128)S(1)}, s32[24,8]{0,1:T(8,128)}, u32[]{:S(2)}) copy-start(s32[24,8]{0,1:T(8,128)} %param.23) | copy-start | bytes 2308
  0.6 13.2 %copy-start.2 = (bf16[24,8]{0,1:T(8,128)(2,1)S(1)}, bf16[24,8]{0,1:T(8,128)(2,1)}, u32[]{:S(2)}) copy-start(bf16[24,8]{0,1:T(8,128)(2,1)} %param.24) | copy-start | bytes 1156
  0.7 13.4 %copy-start = (bf16[24,2048]{1,0:T(8,128)(2,1)S(1)}, bf16[24,2048]{1,0:T(8,128)(2,1)}, u32[]{:S(2)}) copy-start(bf16[24,2048]{1,0:T(8,128)(2,1)} %param.20) | copy-start | bytes 294916

commit v3 on v2

--- a/solution.py
+++ b/solution.py
@@ -92,21 +92,21 @@
 CTX_R, CTX_L, CTX_FR, CTX_FL = 0, 1, 2, 3
 SIDE = 4
 SQUARES = 7
-A_RING_R, A_RING_L = 10, 14
-B_Y = 17
-B_RING_R, B_RING_L = 21, 25
-A_Y = 28
-A_RELAY = 44
-CORE_A = 60
-CORE_B = 64
-S1_R, S1_L, S2_R, S2_L = 72, 80, 88, 96
-H1_R, H1_L, H2_R, H2_L = 104, 112, 120, 128
-CORE_MIX = 136
-CHAIN = 144
-Y_ONE = 152
-Y_TWO = 154
-FINAL = 156
-COPIES = 160
+RING_R, RING_L = 10, 14
+OVER_R, OVER_L = 17, 25
+RELAY = 33
+CORE_ROW = 41
+CORE_SLAB = 49
+S1_R, S1_L, S2_R, S2_L = 52, 60, 68, 76
+H1_R, H1_L, H2_R, H2_L = 84, 92, 100, 108
+CORE_MIX = 116
+CHAIN = 124
+Y_SUM = 152
+FINAL = 155
+COPIES = 158
+
+NEAR = (2, -1, 1, 0)
+FAR = (4, -3, 3, -2)
 
 
 def layer_kernel(
@@ -126,8 +126,7 @@
     down,
     squares,
     attended,
-    rows_a,
-    rows_b,
+    rows,
     picks,
     picked,
     partial,
@@ -139,9 +138,8 @@
     core_in,
     chain_out,
     chain_in,
-    y_part,
-    y_one,
-    y_two,
+    z_sum,
+    y_in,
     final_out,
     final_in,
     send_sem,
@@ -175,7 +173,7 @@
             device_id_type=MESH,
         )
 
-    peers = [x_dev(1), x_dev(2), x_dev(3), y_dev(1), y_dev(3), z_dev(1), z_dev(7), partner]
+    peers = [x_dev(1), x_dev(2), x_dev(3), y_dev(1), y_dev(2), y_dev(3), z_dev(1), z_dev(7), partner]
     barrier = pltpu.get_barrier_semaphore()
     for peer in peers:
         pl.semaphore_signal(barrier, inc=1, device_id=peer, device_id_type=MESH)
@@ -228,10 +226,10 @@
     second = jnp.dot(context, proj[D : 2 * D, :], preferred_element_type=F32)
     for g in range(NX):
         base = g * 2 * DEV_ROWS
-        block = first[base : base + DEV_ROWS] + second[base + DEV_ROWS : base + 2 * DEV_ROWS]
+        term = first[base : base + DEV_ROWS] + second[base + DEV_ROWS : base + 2 * DEV_ROWS]
         residual = side_all[g, 0:32, :].astype(F32)[0:DEV_ROWS]
         attended[g * DEV_ROWS : (g + 1) * DEV_ROWS, :] = (
-            (residual + block).astype(BF16).astype(F32)
+            (residual + term).astype(BF16).astype(F32)
         )
     att = attended[...]
     total = jnp.sum(att * att, axis=1, keepdims=True)
@@ -245,111 +243,26 @@
         + side_all[2, 32:48, 0:HALF].astype(F32)
         + side_all[3, 32:48, 0:HALF].astype(F32)
     )
-    rows_a[core, y, z, COL_ROWS : COL_ROWS + 16, :] = meta.astype(BF16)
+    rows[core, y, z, COL_ROWS : COL_ROWS + 16, 0:HALF] = meta.astype(BF16)
+    rows[core, y, z, COL_ROWS : COL_ROWS + 16, HALF:DQ] = jnp.zeros((16, HALF), BF16)
     for share in shares:
         share.wait_recv()
     total = squares[0][:, 0:1] + squares[1][:, 0:1] + squares[2][:, 0:1] + squares[3][:, 0:1]
     normed = (att * lax.rsqrt(total / D + epsilon) * gain_ref[...]).astype(BF16)
-    rows_a[core, y, z, 0:COL_ROWS, :] = normed[:, 0:HALF]
-    rows_b[core, z, y] = normed[:, HALF:DQ]
-
-    def own_a(where):
-        return rows_a.at[core, y, where]
-
-    b_right = send(rows_b.at[core, z, y], rows_b.at[core, z, y], B_Y, y_dev(1))
-    b_left = send(rows_b.at[core, z, y], rows_b.at[core, z, y], B_Y + 1, y_dev(3))
-    a_right = [send(own_a(z), own_a(z), A_RING_R, z_dev(1))]
-    a_left = [send(own_a(z), own_a(z), A_RING_L, z_dev(7))]
-    a_over = []
-
-    def a_out(where, number):
-        a_over.append(send(own_a(where), own_a(where), A_Y + 2 * number, y_dev(1)))
-        a_over.append(send(own_a(where), own_a(where), A_Y + 2 * number + 1, y_dev(3)))
-
-    a_out(z, 0)
-    y_l, y_r = (y + 3) % NY, (y + 1) % NY
-    top, bottom = pl.ds(0, 48), pl.ds(48, 48)
-    b_right.wait_recv()
-    b_fr = send(rows_b.at[core, z, y_l, top], rows_b.at[core, z, y_l, top], B_Y + 2, y_dev(1))
-    b_left.wait_recv()
-    b_fl = send(
-        rows_b.at[core, z, y_r, bottom], rows_b.at[core, z, y_r, bottom], B_Y + 3, y_dev(3)
-    )
-    a_right[0].wait_recv()
-    left = (z + 7) % NZ
-    a_right.append(send(own_a(left), own_a(left), A_RING_R + 1, z_dev(1)))
-    a_out(left, 1)
-    a_left[0].wait_recv()
-    right = (z + 1) % NZ
-    a_left.append(send(own_a(right), own_a(right), A_RING_L + 1, z_dev(7)))
-    a_out(right, 2)
-    b_fr.wait_recv()
-    b_fl.wait_recv()
-    b_slab = rows_b.at[core, z]
-    z_right = [send(b_slab, b_slab, B_RING_R, z_dev(1))]
-    z_left = [send(b_slab, b_slab, B_RING_L, z_dev(7))]
-    core_copies = [send(b_slab, b_slab, CORE_B, partner)]
-    number = 3
-    for step in (2, 3, 4):
-        a_right[step - 1].wait_recv()
-        left = (z + NZ - step) % NZ
-        if step < 4:
-            a_right.append(send(own_a(left), own_a(left), A_RING_R + step, z_dev(1)))
-        a_out(left, number)
-        number += 1
-        if step < 4:
-            a_left[step - 1].wait_recv()
-            right = (z + step) % NZ
-            if step < 3:
-                a_left.append(send(own_a(right), own_a(right), A_RING_L + step, z_dev(7)))
-            a_out(right, number)
-            number += 1
-    core_copies.append(send(rows_a.at[core, y], rows_a.at[core, y], CORE_A, partner))
-
-    def a_relay(number, where):
-        a_over[2 * number].wait_recv()
-        a_over[2 * number + 1].wait_recv()
-        if number % 2 == 0:
-            block = rows_a.at[core, y_l, where]
-            return send(block, block, A_RELAY + number, y_dev(1))
-        block = rows_a.at[core, y_r, where]
-        return send(block, block, A_RELAY + number, y_dev(3))
-
-    order = [z, (z + 7) % NZ, (z + 1) % NZ, (z + 6) % NZ, (z + 2) % NZ, (z + 5) % NZ]
-    order += [(z + 3) % NZ, (z + 4) % NZ]
-    relays = []
-    for step in (1, 2, 3, 4):
-        z_right[step - 1].wait_recv()
-        slab = rows_b.at[core, (z + NZ - step) % NZ]
-        if step < 4:
-            z_right.append(send(slab, slab, B_RING_R + step, z_dev(1)))
-        core_copies.append(send(slab, slab, CORE_B + 2 * step - 1, partner))
-        for number in (2 * step - 2, 2 * step - 1):
-            relays.append(a_relay(number, order[number]))
-        if step < 4:
-            z_left[step - 1].wait_recv()
-            slab = rows_b.at[core, (z + step) % NZ]
-            if step < 3:
-                z_left.append(send(slab, slab, B_RING_L + step, z_dev(7)))
-            core_copies.append(send(slab, slab, CORE_B + 2 * step, partner))
-    for there, number in ((y_l, 1), (y_r, 2)):
-        slab = rows_a.at[core, there]
-        core_copies.append(send(slab, slab, CORE_A + number, partner))
-    for relay in relays:
-        relay.wait_recv()
-    slab = rows_a.at[core, (y + 2) % NY]
-    core_copies.append(send(slab, slab, CORE_A + 3, partner))
-    for made in core_copies:
-        made.wait_recv()
+    rows[core, y, z, 0:COL_ROWS, :] = normed
     loads[1].wait()
     loads[2].wait()
 
     opposite = (x + 2) % NX
     lower, upper = pl.ds(0, FF), pl.ds(FF, FF)
 
-    def chunk_of(k):
-        odd = k % 2
-        return (z + NZ + (1 - odd) * (4 - k // 2) + odd * (k // 2 - 3)) % NZ
+    def group_of(k):
+        u = k // 2
+        return (y + u + 2 * (u % 2) * (1 - u // 2) - u // 2) % NY
+
+    def z_of(k, o):
+        near = (k + 1 - (k // 2 + 3) // 4) % 2
+        return (z + NZ + near * NEAR[o] + (1 - near) * FAR[o]) % NZ
 
     def first_copies(k):
         return (
@@ -380,22 +293,17 @@
     def core_copy(k):
         return copy(mixed.at[k, 1 - core], core_in.at[k], CORE_MIX + k, partner)
 
-    def chain_right(k):
-        return copy(chain_out.at[k], chain_in.at[k], CHAIN + k, z_dev(1))
-
-    def chain_left(k):
-        return copy(chain_out.at[k], chain_in.at[k], CHAIN + k, z_dev(7))
-
     row_iota = lax.broadcasted_iota(jnp.int32, (COL_ROWS, COL_ROWS), 0)
     lane_iota = lax.broadcasted_iota(jnp.int32, (COL_ROWS, COL_ROWS), 1)
     earlier = (row_iota < lane_iota).astype(F32).astype(BF16)
     place = lax.broadcasted_iota(jnp.int32, (SPAN, COL_ROWS), 0).astype(F32)
 
     def pick_and_multiply(k):
-        g = chunk_of(k)
+        group = group_of(k)
         for column in range(2 * NY):
-            cy, cc = column // 2, column % 2
-            meta = rows_a[cc, cy, g, COL_ROWS : COL_ROWS + 16, :].astype(F32)[:, 0:COL_ROWS]
+            there, cc = z_of(k, column // 2), column % 2
+            meta = rows[cc, group, there, COL_ROWS : COL_ROWS + 16, 0:128].astype(F32)
+            meta = meta[:, 0:COL_ROWS]
             ids, weights = meta[0:TOPK], meta[TOPK : 2 * TOPK]
             scale = 1.0 / jnp.sum(weights, axis=0, keepdims=True)
             named, share = [], []
@@ -422,12 +330,9 @@
                 weighted.append(pick * share[j])
             pick = jnp.concatenate(chosen, axis=0).astype(BF16)
             picks[k % 8, column] = jnp.concatenate(weighted, axis=0)
-            got_a = jnp.dot(pick, rows_a[cc, cy, g, 0:COL_ROWS, :], preferred_element_type=F32)
-            got_b = jnp.dot(pick, rows_b[cc, g, cy], preferred_element_type=F32)
+            got = jnp.dot(pick, rows[cc, group, there, 0:COL_ROWS, :], preferred_element_type=F32)
             for j in range(SLOTS_DEV):
-                span = slice(j * SPAN, (j + 1) * SPAN)
-                picked[j, column * SPAN : (column + 1) * SPAN, 0:HALF] = got_a[span]
-                picked[j, column * SPAN : (column + 1) * SPAN, HALF:DQ] = got_b[span]
+                picked[j, column * SPAN : (column + 1) * SPAN, :] = got[j * SPAN : (j + 1) * SPAN]
         for j in range(SLOTS_DEV):
             inputs = picked[j].astype(BF16)
             for part in range(3):
@@ -476,7 +381,7 @@
             product = jnp.dot(inputs, down[j], preferred_element_type=F32)
             expert_out[j] = product.astype(BF16).astype(F32)
         for column in range(2 * NY):
-            cy, cc = column // 2, column % 2
+            cc = column % 2
             span = slice(column * SPAN, (column + 1) * SPAN)
             results = jnp.concatenate([expert_out[j, span] for j in range(SLOTS_DEV)], axis=0)
             mixture = lax.dot_general(
@@ -485,65 +390,175 @@
                 (((0,), (0,)), ((), ())),
                 preferred_element_type=F32,
             )
-            mixed[k, cc, cy] = mixture.astype(BF16)
+            mixed[k, cc, column // 2] = mixture.astype(BF16)
         core_copy(k).start()
 
-    def chain(k):
+    def chunk_with(group, offset):
+        near = offset in NEAR
+        index = (NEAR if near else FAR).index(offset)
+        first_half = near if group == 0 else not near
+        return 2 * group + (0 if first_half else 1), index
+
+    def chain_copy(group, leg, step):
+        index = leg * 4 + step
+        device = z_dev(1) if leg == 0 else z_dev(7)
+        return copy(
+            chain_out.at[group, index],
+            chain_in.at[group, index],
+            CHAIN + 7 * group + index,
+            device,
+        )
+
+    def block(group, offset):
+        k, index = chunk_with(group, offset)
+        return mixed[k, core, index].astype(F32) + core_in[k, index].astype(F32)
+
+    def chain(group, step):
+        for leg, offset in ((0, 4 - step), (1, step - 3)):
+            if offset == 0:
+                continue
+            value = block(group, offset)
+            if step > 0:
+                chain_copy(group, leg, step - 1).wait_recv()
+                value = value + chain_in[group, leg * 4 + step - 1].astype(F32)
+            chain_out[group, leg * 4 + step] = value.astype(BF16)
+            chain_copy(group, leg, step).start()
+
+    def y_copy(group):
+        step = (0, 3, 1, 2)[group]
+        return copy(z_sum.at[group], y_in.at[group - 1], Y_SUM + group - 1, y_dev(step))
+
+    def close(group):
+        chain_copy(group, 1, 2).wait_recv()
+        chain_copy(group, 0, 3).wait_recv()
+        value = block(group, 0)
+        value = value + chain_in[group, 3].astype(F32) + chain_in[group, 6].astype(F32)
+        z_sum[group] = value.astype(BF16)
+        if group > 0:
+            y_copy(group).start()
+
+    y_l, y_r = (y + 3) % NY, (y + 1) % NY
+
+    def own_row(where):
+        return rows.at[core, y, where % NZ]
+
+    def ring(leg, step):
+        where, device = (z + NZ - step, z_dev(1)) if leg == 0 else (z + step, z_dev(7))
+        index = (RING_R if leg == 0 else RING_L) + step
+        return copy(own_row(where), own_row(where), index, device)
+
+    arrivals = (0, -1, 1, -2, 2, -3, 3, 4)
+
+    def over(number, leg):
+        block_ref = own_row(z + NZ + arrivals[number])
+        index = (OVER_R if leg == 0 else OVER_L) + number
+        return copy(block_ref, block_ref, index, y_dev(1) if leg == 0 else y_dev(3))
+
+    def relay(number):
+        where = (z + NZ + arrivals[number]) % NZ
+        block_ref = rows.at[core, y_l if number % 2 == 0 else y_r, where]
+        return copy(block_ref, block_ref, RELAY + number, y_dev(1) if number % 2 == 0 else y_dev(3))
+
+    def core_row(number):
+        block_ref = own_row(z + NZ + arrivals[number])
+        return copy(block_ref, block_ref, CORE_ROW + number, partner)
+
+    def core_slab(group):
+        slab = rows.at[core, (y + (0, 3, 1, 2)[group]) % NY]
+        return copy(slab, slab, CORE_SLAB + group - 1, partner)
+
+    def spread(number):
+        core_row(number).start()
+        over(number, 0).start()
+        over(number, 1).start()
+
+    ring(0, 0).start()
+    ring(1, 0).start()
+    spread(0)
+    for step in (1, 2):
+        ring(1, step - 1).wait_recv()
+        if step < 3:
+            ring(1, step).start()
+        spread(2 * step)
+        ring(0, step - 1).wait_recv()
+        ring(0, step).start()
+        spread(2 * step - 1)
+    for number in (0, 1, 2, 4):
+        core_row(number).wait_recv()
+    pick_and_multiply(0)
+    ring(1, 2).wait_recv()
+    spread(6)
+    ring(0, 2).wait_recv()
+    ring(0, 3).start()
+    spread(5)
+    ring(0, 3).wait_recv()
+    spread(7)
+
+    def receive_left():
+        for number in range(NZ):
+            over(number, 0).wait_recv()
+            if number % 2 == 0:
+                relay(number).start()
+        core_slab(1).start()
+
+    def receive_right():
+        for number in range(NZ):
+            over(number, 1).wait_recv()
+            if number % 2 == 1:
+                relay(number).start()
+        core_slab(2).start()
+
+    def receive_far():
+        for number in range(NZ):
+            relay(number).wait_recv()
+        core_slab(3).start()
+
+    events = {
+        1: [receive_left],
+        2: [receive_right],
+        4: [receive_far],
+    }
+    ready = {
+        1: [functools.partial(lambda n: core_row(n).wait_recv(), n) for n in (3, 5, 6, 7)],
+        2: [lambda: core_slab(1).wait_recv()],
+        4: [lambda: core_slab(2).wait_recv()],
+        6: [lambda: core_slab(3).wait_recv()],
+    }
+    chains = {}
+    for group in range(NY):
+        start = 2 * group + 5 + (group == 0)
+        for step in range(4):
+            chains.setdefault(start + step, []).append(functools.partial(chain, group, step))
+        chains.setdefault(start + 4, []).append(functools.partial(close, group))
+
+    def at(t, table):
+        for when, works in table.items():
+
+            @pl.when(t == when)
+            def _(works=works):
+                for work in works:
+                    work()
+
+    def core_arrived(k):
         core_copy(k).wait_recv()
 
-        @pl.when(k < 2)
-        def _():
-            chain_out[k] = (mixed[k, core].astype(F32) + core_in[k].astype(F32)).astype(BF16)
-
-        @pl.when((k >= 2) & (k < NZ - 1))
-        def _():
-            chain_right(k - 2).wait_recv()
-            chain_out[k] = (
-                mixed[k, core].astype(F32) + core_in[k].astype(F32) + chain_in[k - 2].astype(F32)
-            ).astype(BF16)
-
-        @pl.when((k < NZ - 1) & (k % 2 == 0))
-        def _():
-            chain_right(k).start()
-
-        @pl.when((k < NZ - 1) & (k % 2 == 1))
-        def _():
-            chain_left(k).start()
-
     def tick(t, carry):
-        for stage, work in ((5, chain), (4, mix), (3, pass_hidden), (2, add_second), (1, add_first)):
+        pl.when((t >= 5) & (t < NZ + 5))(functools.partial(core_arrived, t - 5))
+        at(t, chains)
+        for stage, work in ((4, mix), (3, pass_hidden), (2, add_second), (1, add_first)):
             pl.when((t >= stage) & (t < NZ + stage))(functools.partial(work, t - stage))
+        at(t, ready)
         pl.when(t < NZ)(functools.partial(pick_and_multiply, t))
+        at(t, events)
         return carry
 
-    lax.fori_loop(0, NZ + 6, tick, 0)
-
-    last = NZ - 1
-    chain_right(last - 2).wait_recv()
-    chain_right(last - 1).wait_recv()
-    for there in range(NY):
-        y_part[there] = (
-            mixed[last, core, there].astype(F32)
-            + core_in[last, there].astype(F32)
-            + chain_in[last - 2, there].astype(F32)
-            + chain_in[last - 1, there].astype(F32)
-        ).astype(BF16)
-    y_far = (y + 2) % NY
-    one_r = send(y_part.at[y_far, top], y_one.at[0], Y_ONE, y_dev(1))
-    one_l = send(y_part.at[y_far, bottom], y_one.at[1], Y_ONE + 1, y_dev(3))
-    one_r.wait_recv()
-    y_part[y_r, 0:48, :] = (
-        y_part[y_r, 0:48, :].astype(F32) + y_one[0].astype(F32)
-    ).astype(BF16)
-    two_r = send(y_part.at[y_r], y_two.at[0], Y_TWO, y_dev(1))
-    one_l.wait_recv()
-    y_part[y_l, 48:96, :] = (
-        y_part[y_l, 48:96, :].astype(F32) + y_one[1].astype(F32)
-    ).astype(BF16)
-    two_l = send(y_part.at[y_l], y_two.at[1], Y_TWO + 1, y_dev(3))
-    two_r.wait_recv()
-    two_l.wait_recv()
-    mixture = y_part[y].astype(F32) + y_two[0].astype(F32) + y_two[1].astype(F32)
+    lax.fori_loop(1, max(chains) + 1, tick, 0)
+
+    for group in range(1, NY):
+        y_copy(group).wait_recv()
+    mixture = z_sum[0].astype(F32)
+    for group in range(1, NY):
+        mixture = mixture + y_in[group - 1].astype(F32)
     both = attended[...] + mixture
     for g in range(NX):
         span = slice(g * DEV_ROWS, (g + 1) * DEV_ROWS)
@@ -556,10 +571,10 @@
     for made in finals:
         made.wait_recv()
     for g in range(NX):
-        block = final_in[g].astype(F32)
+        ended = final_in[g].astype(F32)
         lanes = slice(g * DQ, (g + 1) * DQ)
-        moe_ref[:, lanes] = block[0:DEV_ROWS].astype(BF16)
-        layer_ref[:, lanes] = block[DEV_ROWS : 2 * DEV_ROWS].astype(BF16)
+        moe_ref[:, lanes] = ended[0:DEV_ROWS].astype(BF16)
+        layer_ref[:, lanes] = ended[DEV_ROWS : 2 * DEV_ROWS].astype(BF16)
 
     def drain(k, carry):
         for made in (
@@ -571,13 +586,24 @@
         ):
             made.wait_send()
 
-        @pl.when(k < NZ - 1)
-        def _():
-            chain_right(k).wait_send()
-
         return carry
 
     lax.fori_loop(0, NZ, drain, 0)
+    for step in range(4):
+        ring(0, step).wait_send()
+        if step < 3:
+            ring(1, step).wait_send()
+    for number in range(NZ):
+        for made in (over(number, 0), over(number, 1), relay(number), core_row(number)):
+            made.wait_send()
+    for group in range(NY):
+        for step in range(4):
+            chain_copy(group, 0, step).wait_send()
+            if step < 3:
+                chain_copy(group, 1, step).wait_send()
+        if group > 0:
+            core_slab(group).wait_send()
+            y_copy(group).wait_send()
     for made in pending:
         made.wait_send()
 
@@ -601,8 +627,7 @@
             pltpu.VMEM((SLOTS_DEV, FF, DQ), BF16),
             pltpu.VMEM((NX, COL_ROWS, 128), F32),
             pltpu.VMEM((COL_ROWS, DQ), F32),
-            pltpu.VMEM((2, NY, NZ, COL_ROWS + 16, HALF), BF16),
-            pltpu.VMEM((2, NZ, NY, COL_ROWS, HALF), BF16),
+            pltpu.VMEM((2, NY, NZ, COL_ROWS + 16, DQ), BF16),
             pltpu.VMEM((NZ, 2 * NY, SLOTS_DEV * SPAN, COL_ROWS), F32),
             pltpu.VMEM((SLOTS_DEV, 2 * NY * SPAN, DQ), F32),
             pltpu.VMEM((NZ, NX, 48, 2 * FF), BF16),
@@ -612,11 +637,10 @@
             pltpu.VMEM((SLOTS_DEV, 2 * NY * SPAN, DQ), F32),
             pltpu.VMEM((NZ, 2, NY, COL_ROWS, DQ), BF16),
             pltpu.VMEM((NZ, NY, COL_ROWS, DQ), BF16),
-            pltpu.VMEM((NZ, NY, COL_ROWS, DQ), BF16),
-            pltpu.VMEM((NZ, NY, COL_ROWS, DQ), BF16),
+            pltpu.VMEM((NY, 7, COL_ROWS, DQ), BF16),
+            pltpu.VMEM((NY, 7, COL_ROWS, DQ), BF16),
             pltpu.VMEM((NY, COL_ROWS, DQ), BF16),
-            pltpu.VMEM((2, COL_ROWS // 2, DQ), BF16),
-            pltpu.VMEM((2, COL_ROWS, DQ), BF16),
+            pltpu.VMEM((NY - 1, COL_ROWS, DQ), BF16),
             pltpu.VMEM((NX, 48, DQ), BF16),
             pltpu.VMEM((NX, 48, DQ), BF16),
             pltpu.SemaphoreType.DMA((COPIES,)),

time: 177 us -> 157 us (0.89)
  Pallas kernels: 158 us -> 138 us
    pallas_call x1, Pallas kernels: 158 us -> 138 us  [whole_layer(): pl.pallas_call(layer_kernel, out_shape=(jax.ShapeDtypeStruct((DEV_ROWS, D...]
where the time goes in v3:
time: 157 us; the launch traced here: 156 us
  Pallas kernels  138 us (88%)
  local copies, waits for them, and re-layouts  6.5 us (4%)
  matrix products  5.54 us (4%)
  other arithmetic  5.01 us (3%)
    pallas_call x1, Pallas kernels, whole_layer(): pl.pallas_call(layer_kernel, out_shape=(jax.ShapeDtypeStruct((DEV_ROWS, D...  138 us
    unnamed x12, local copies, waits for them, and re-layouts  4.93 us

profile of v3, /device:TPU:32, one launch (start us, length us, event | category | flops | bytes accessed | tf_op | source)
XLA Modules:
  0.0 156.1 jit_solution(16466682523802667613)
XLA Ops:
  0.7 0.8 broadcast_add_fusion
  1.5 0.9 fusion.30
  2.4 0.1 add_convert_fusion.1
  2.5 0.7 broadcast_in_dim.32.table_ref
  3.1 0.9 slice_bitcast_fusion
  4.1 0.7 iota_compare_fusion.3
  4.8 1.7 %fusion.42 = (f32[16,4,8]{2,1,0:T(4,128)S(1)}, f32[16,4,8,48]{3,2,1,0:T(8,128)S(1)}) fusion(bf16[16,4,8,128]{3,2,1,0:T(8,128)(2,1)S(1)} %bitcast.84, pred[16,48]{1,0:T(8,128)(4,1)S(1)} %iota_compare_fusion.3, bf16[16,48,512]{2,1,0:T(8,128)(2,1)} %param.17), kind=kOutput, calls=%fused_computation.68 | convolution fusion | flops 6364672 | bytes 1018624 | tf_op jit(solution)/shard_map/nkgd,ntkd->nkgt/dot_general | solution.py:67
  6.5 0.7 slice.28
  7.3 0.2 fusion.48
  7.5 0.3 fusion.12
  7.9 0.7 slice_convert_fusion
  8.6 1.5 fusion.2
  10.1 0.1 copy.63
  10.2 0.8 slice_bitcast_fusion.1
  11.0 1.1 fusion.43
  12.2 0.1 copy.25
  12.3 0.8 convolution_convert_fusion
  13.2 0.7 fusion.14.ctx_ref
  13.9 0.0 copy-done.2
  13.9 0.1 convolution_convert_fusion.1
  14.0 0.7 fusion.13.side_ref
  14.7 138.2 %shard_map.149 = (bf16[24,2048]{1,0:T(8,128)(2,1)}, bf16[24,2048]{1,0:T(8,128)(2,1)}) custom-call(bf16[48,2048]{1,0:T(8,128)(2,1)} %fusion.14.ctx_ref, bf16[4,48,512]{2,1,0:T(8,128)(2,1)} %fusion.13.side_ref, bf16[4096,512]{1,0:T(8,128)(2,1)} %out_proj_hbm.1, f32[1,512]{1,0:T(1,128)} %bitcast.91, f32[16,128]{1,0:T(8,128)} %broadcast_in_dim.32.table_ref, ...), custom_call_target="tpu_custom_call" | custom-call | tf_op jit(solution)/shard_map/pallas_call | solution.py:614
  153.0 1.5 copy.67
  154.5 1.5 copy.68
  (20 shorter events, 0.2 us)
Async XLA Ops:
  0.6 13.2 %copy-start.1 = (s32[24,8]{0,1:T(8,128)S(1)}, s32[24,8]{0,1:T(8,128)}, u32[]{:S(2)}) copy-start(s32[24,8]{0,1:T(8,128)} %param.23) | copy-start | bytes 2308
  0.6 13.2 %copy-start.2 = (bf16[24,8]{0,1:T(8,128)(2,1)S(1)}, bf16[24,8]{0,1:T(8,128)(2,1)}, u32[]{:S(2)}) copy-start(bf16[24,8]{0,1:T(8,128)(2,1)} %param.24) | copy-start | bytes 1156
  0.7 13.4 %copy-start = (bf16[24,2048]{1,0:T(8,128)(2,1)S(1)}, bf16[24,2048]{1,0:T(8,128)(2,1)}, u32[]{:S(2)}) copy-start(bf16[24,2048]{1,0:T(8,128)(2,1)} %param.20) | copy-start | bytes 294916

commit v4 on v3

--- a/solution.py
+++ b/solution.py
@@ -32,63 +32,6 @@
 masked_score = -1e30
 epsilon = 1e-06
 
-
-def prefill_context(queries, new_keys, new_values):
-    head_group = HEADS // KV_HEADS
-    scaling = 1.0 / math.sqrt(HEAD_DIM)
-    query_pre = queries[:PRE].reshape(PRE, KV_HEADS, head_group, HEAD_DIM)
-    keys_pre = new_keys[:PRE].reshape(PRE, KV_HEADS, HEAD_DIM)
-    values_pre = new_values[:PRE].reshape(PRE, KV_HEADS, HEAD_DIM)
-    scores = (
-        jnp.einsum("ikgd,jkd->kgij", query_pre, keys_pre, preferred_element_type=jnp.float32)
-        * scaling
-    )
-    causal = jnp.arange(PRE)[:, None] >= jnp.arange(PRE)[None, :]
-    scores = jnp.where(causal, scores, masked_score)
-    exponent = jnp.exp(scores - jnp.max(scores, axis=-1, keepdims=True))
-    attn_probs = (exponent / jnp.sum(exponent, axis=-1, keepdims=True)).astype(jnp.bfloat16)
-    mixed_values = jnp.einsum(
-        "kgij,jkd->ikgd", attn_probs, values_pre, preferred_element_type=jnp.float32
-    )
-    return mixed_values.astype(jnp.bfloat16).reshape(PRE, HEADS * HEAD_DIM)
-
-
-def decode_context(queries, new_keys, new_values, key_cache, value_cache, cache_len):
-    requests = key_cache.shape[0]
-    cache_slots = key_cache.shape[1]
-    head_group = HEADS // KV_HEADS
-    scaling = 1.0 / math.sqrt(HEAD_DIM)
-    query_dec = queries[PRE:].reshape(requests, KV_HEADS, head_group, HEAD_DIM)
-    keys_dec = new_keys[PRE:].reshape(requests, KV_HEADS, HEAD_DIM)
-    values_dec = new_values[PRE:].reshape(requests, KV_HEADS, HEAD_DIM)
-    cached_keys = key_cache.reshape(requests, cache_slots, KV_HEADS, HEAD_DIM)
-    cached_values = value_cache.reshape(requests, cache_slots, KV_HEADS, HEAD_DIM)
-    cache_scores = (
-        jnp.einsum("nkgd,ntkd->nkgt", query_dec, cached_keys, preferred_element_type=jnp.float32)
-        * scaling
-    )
-    own_score = (
-        jnp.einsum("nkgd,nkd->nkg", query_dec, keys_dec, preferred_element_type=jnp.float32)
-        * scaling
-    )
-    valid = jnp.arange(cache_slots)[None, :] < cache_len[:, None]
-    cache_scores = jnp.where(valid[:, None, None, :], cache_scores, masked_score)
-    top_score = jnp.maximum(jnp.max(cache_scores, axis=-1), own_score)
-    cache_exp = jnp.exp(cache_scores - top_score[..., None])
-    own_exp = jnp.exp(own_score - top_score)
-    denominator = jnp.sum(cache_exp, axis=-1) + own_exp
-    cache_probs = (cache_exp / denominator[..., None]).astype(jnp.bfloat16)
-    own_probs = (own_exp / denominator).astype(jnp.bfloat16)
-    mixed_values = jnp.einsum(
-        "nkgt,ntkd->nkgd", cache_probs, cached_values, preferred_element_type=jnp.float32
-    )
-    mixed_values = (
-        mixed_values
-        + own_probs.astype(jnp.float32)[..., None] * values_dec.astype(jnp.float32)[:, :, None, :]
-    )
-    return mixed_values.astype(jnp.bfloat16).reshape(requests, HEADS * HEAD_DIM)
-
-
 CTX_R, CTX_L, CTX_FR, CTX_FL = 0, 1, 2, 3
 SIDE = 4
 SQUARES = 7
@@ -110,15 +53,34 @@
 
 
 def layer_kernel(
-    ctx_ref,
-    side_ref,
+    queries_hbm,
+    new_keys_hbm,
+    new_values_hbm,
+    key_cache_hbm,
+    value_cache_hbm,
+    cache_len_ref,
+    residual_hbm,
     out_proj_hbm,
     gain_ref,
-    table_ref,
+    ids_ref,
+    weights_ref,
+    slots_ref,
     gate_up_hbm,
     down_hbm,
     moe_ref,
     layer_ref,
+    queries,
+    new_keys,
+    new_values,
+    key_cache,
+    value_cache,
+    residual,
+    by_head,
+    context_head,
+    own_keys,
+    own_values,
+    table_ref,
+    side_out,
     ctx_all,
     side_all,
     proj,
@@ -178,15 +140,124 @@
     for peer in peers:
         pl.semaphore_signal(barrier, inc=1, device_id=peer, device_id_type=MESH)
 
+    early = [
+        pltpu.make_async_copy(queries_hbm, queries, load_sem.at[0]),
+        pltpu.make_async_copy(new_keys_hbm, new_keys, load_sem.at[1]),
+        pltpu.make_async_copy(new_values_hbm, new_values, load_sem.at[2]),
+        pltpu.make_async_copy(key_cache_hbm, key_cache, load_sem.at[3]),
+        pltpu.make_async_copy(value_cache_hbm, value_cache, load_sem.at[4]),
+        pltpu.make_async_copy(residual_hbm, residual, load_sem.at[5]),
+    ]
     loads = [
-        pltpu.make_async_copy(out_proj_hbm, proj, load_sem.at[0]),
-        pltpu.make_async_copy(gate_up_hbm, gate_up, load_sem.at[1]),
-        pltpu.make_async_copy(down_hbm, down, load_sem.at[2]),
-        pltpu.make_async_copy(ctx_ref, ctx_all.at[x], load_sem.at[3]),
-        pltpu.make_async_copy(side_ref.at[x], side_all.at[x], load_sem.at[4]),
+        pltpu.make_async_copy(out_proj_hbm, proj, load_sem.at[6]),
+        pltpu.make_async_copy(gate_up_hbm, gate_up, load_sem.at[7]),
+        pltpu.make_async_copy(down_hbm, down, load_sem.at[8]),
     ]
-    for load in loads:
+    for load in early + loads:
         load.start()
+
+    slots = slots_ref[...].astype(F32)
+    slot_lane = lax.broadcasted_iota(jnp.int32, slots.shape, 1)
+    for j in range(SLOTS_DEV):
+        here = ep * SLOTS_DEV + j
+        mine = jnp.sum(jnp.where(slot_lane == here, slots, 0.0), axis=1, keepdims=True)
+        same = jnp.where(slots == mine, 1.0, 0.0)
+        twice = jnp.sum(same, axis=1, keepdims=True) - 1.0
+        before = jnp.sum(jnp.where(slot_lane < here, same, 0.0), axis=1, keepdims=True)
+        for row, value in ((j, mine + 1.0), (3 + j, twice), (6 + j, before)):
+            table_ref[row : row + 1, :] = jnp.broadcast_to(value, (1, 128))
+    spread_row = lax.broadcasted_iota(jnp.int32, (DEV_ROWS, HALF), 0)
+    spread_lane = lax.broadcasted_iota(jnp.int32, (DEV_ROWS, HALF), 1)
+    to_lane = jnp.where(spread_lane == spread_row + x * DEV_ROWS, 1.0, 0.0).astype(BF16)
+    routes = [
+        lax.dot_general(
+            value.astype(BF16), to_lane, (((0,), (0,)), ((), ())), preferred_element_type=F32
+        )
+        for value in (ids_ref[...].astype(F32) + 1.0, weights_ref[...].astype(F32))
+    ]
+    routes = jnp.concatenate(routes, axis=0).astype(BF16)
+    for load in early:
+        load.wait()
+    for g in range(NX):
+        side_out[g, 0:DEV_ROWS, :] = residual[:, g * DQ : (g + 1) * DQ]
+        side_out[g, 32:48, 0:HALF] = routes
+
+    own_keys[...] = new_keys[...].astype(F32)
+    own_values[...] = new_values[...].astype(F32)
+    for h in range(HEADS):
+        by_head[pl.ds(h, DEV_ROWS, stride=HEADS), :] = queries[
+            :, h * HEAD_DIM : (h + 1) * HEAD_DIM
+        ].astype(F32)
+    width = KV_HEADS * HEAD_DIM
+    head_row = lax.broadcasted_iota(jnp.int32, (HEADS, width), 0)
+    head_lane = lax.broadcasted_iota(jnp.int32, (HEADS, width), 1)
+    same_head = head_row // (HEADS // KV_HEADS) == head_lane // HEAD_DIM
+    scaling = 1.0 / math.sqrt(HEAD_DIM)
+
+    def spread_query(row):
+        query = by_head[pl.ds(row * HEADS, HEADS), :]
+        return jnp.where(same_head, jnp.concatenate([query] * KV_HEADS, axis=1), 0.0)
+
+    def join(mixed_values):
+        mixed_values = jnp.where(same_head, mixed_values, 0.0)
+        joined = mixed_values[:, 0:HEAD_DIM]
+        for kv in range(1, KV_HEADS):
+            joined = joined + mixed_values[:, kv * HEAD_DIM : (kv + 1) * HEAD_DIM]
+        return joined
+
+    def score(query, keys):
+        return (
+            lax.dot_general(
+                query.astype(BF16), keys, (((1,), (1,)), ((), ())), preferred_element_type=F32
+            )
+            * scaling
+        )
+
+    def prefill_row(row):
+        query = spread_query(row)
+        scores = score(query, new_keys[0 : 2 * PRE, :])
+        token = lax.broadcasted_iota(jnp.int32, scores.shape, 1)
+        scores = jnp.where(token <= row, scores, masked_score)
+        exponent = jnp.exp(scores - jnp.max(scores, axis=1, keepdims=True))
+        probs = (exponent / jnp.sum(exponent, axis=1, keepdims=True)).astype(BF16)
+        values = jnp.dot(probs, new_values[0 : 2 * PRE, :], preferred_element_type=F32)
+        context_head[pl.ds(row * HEADS, HEADS), :] = join(values)
+
+    def decode_row(request):
+        row = PRE + request
+        query = spread_query(row)
+        scores = score(query, key_cache[request])
+        token = lax.broadcasted_iota(jnp.int32, scores.shape, 1)
+        scores = jnp.where(token < cache_len_ref[request], scores, masked_score)
+        own = jnp.sum(query * own_keys[pl.ds(row, 1), :], axis=1, keepdims=True) * scaling
+        top = jnp.maximum(jnp.max(scores, axis=1, keepdims=True), own)
+        exponent = jnp.exp(scores - top)
+        own_exp = jnp.exp(own - top)
+        total = jnp.sum(exponent, axis=1, keepdims=True) + own_exp
+        probs = (exponent / total).astype(BF16)
+        own_prob = (own_exp / total).astype(BF16).astype(F32)
+        values = jnp.dot(probs, value_cache[request], preferred_element_type=F32)
+        values = values + own_prob * own_values[pl.ds(row, 1), :]
+        context_head[pl.ds(row * HEADS, HEADS), :] = join(values)
+
+    def four(work):
+        def body(i, carry):
+            for part in range(4):
+                work(i * 4 + part)
+            return carry
+
+        return body
+
+    lax.fori_loop(0, PRE // 4, four(prefill_row), 0)
+    lax.fori_loop(0, (DEV_ROWS - PRE) // 4, four(decode_row), 0)
+    for h in range(HEADS // 2):
+        pair = [
+            context_head[pl.ds(there, DEV_ROWS, stride=HEADS), :] for there in (h, h + HEADS // 2)
+        ]
+        ctx_all[x, :, h * HEAD_DIM : (h + 1) * HEAD_DIM] = jnp.concatenate(pair, axis=0).astype(
+            BF16
+        )
+    side_all[x] = side_out[x]
     pl.semaphore_wait(barrier, len(peers))
 
     pending = []
@@ -197,12 +268,12 @@
         pending.append(made)
         return made
 
-    ctx_r = send(ctx_ref, ctx_all.at[x], CTX_R, x_dev(1))
-    ctx_l = send(ctx_ref, ctx_all.at[x], CTX_L, x_dev(3))
+    ctx_r = send(ctx_all.at[x], ctx_all.at[x], CTX_R, x_dev(1))
+    ctx_l = send(ctx_all.at[x], ctx_all.at[x], CTX_L, x_dev(3))
     sides = []
     for step in (1, 2, 3):
         there = (x + step) % NX
-        sides.append(send(side_ref.at[there], side_all.at[x], SIDE + step - 1, x_dev(step)))
+        sides.append(send(side_out.at[there], side_all.at[x], SIDE + step - 1, x_dev(step)))
     from_l, from_r = (x + 3) % NX, (x + 1) % NX
     ctx_r.wait_recv()
     low, high = pl.ds(0, D // 2), pl.ds(D // 2, D // 2)
@@ -214,8 +285,6 @@
         ctx_all.at[from_r, :, high], ctx_all.at[from_r, :, high], CTX_FL, x_dev(3)
     )
     loads[0].wait()
-    loads[3].wait()
-    loads[4].wait()
     for side in sides:
         side.wait_recv()
     fwd_r.wait_recv()
@@ -608,18 +677,47 @@
         made.wait_send()
 
 
-def whole_layer(ctx, side, out_proj, gain, table, gate_up, down_proj):
+def local(
+    queries,
+    new_keys,
+    new_values,
+    key_cache,
+    value_cache,
+    cache_len,
+    residual,
+    out_proj,
+    norm_gain,
+    expert_ids,
+    route_weights,
+    slot_expert,
+    gate_up,
+    down_proj,
+):
     vmem = pl.BlockSpec(memory_space=pltpu.VMEM)
+    smem = pl.BlockSpec(memory_space=pltpu.SMEM)
     hbm = pl.BlockSpec(memory_space=pl.ANY)
+    requests, cached, width = key_cache.shape
     return pl.pallas_call(
         layer_kernel,
         out_shape=(
             jax.ShapeDtypeStruct((DEV_ROWS, D), BF16),
             jax.ShapeDtypeStruct((DEV_ROWS, D), BF16),
         ),
-        in_specs=[vmem, vmem, hbm, vmem, vmem, hbm, hbm],
+        in_specs=[hbm] * 5 + [smem] + [hbm] * 2 + [vmem] * 4 + [hbm] * 2,
         out_specs=(vmem, vmem),
         scratch_shapes=[
+            pltpu.VMEM((DEV_ROWS, 2 * D), BF16),
+            pltpu.VMEM((DEV_ROWS, width), BF16),
+            pltpu.VMEM((DEV_ROWS, width), BF16),
+            pltpu.VMEM((requests, cached, width), BF16),
+            pltpu.VMEM((requests, cached, width), BF16),
+            pltpu.VMEM((DEV_ROWS, D), BF16),
+            pltpu.VMEM((DEV_ROWS * HEADS, HEAD_DIM), F32),
+            pltpu.VMEM((DEV_ROWS * HEADS, HEAD_DIM), F32),
+            pltpu.VMEM((DEV_ROWS, width), F32),
+            pltpu.VMEM((DEV_ROWS, width), F32),
+            pltpu.VMEM((16, 128), F32),
+            pltpu.VMEM((NX, 48, DQ), BF16),
             pltpu.VMEM((NX, 2 * DEV_ROWS, D), BF16),
             pltpu.VMEM((NX, 48, DQ), BF16),
             pltpu.VMEM((2 * D, DQ), BF16),
@@ -645,58 +743,27 @@
             pltpu.VMEM((NX, 48, DQ), BF16),
             pltpu.SemaphoreType.DMA((COPIES,)),
             pltpu.SemaphoreType.DMA((COPIES,)),
-            pltpu.SemaphoreType.DMA((5,)),
+            pltpu.SemaphoreType.DMA((9,)),
         ],
         compiler_params=pltpu.CompilerParams(
             collective_id=0, has_side_effects=True, vmem_limit_bytes=67043328
         ),
-    )(ctx, side, out_proj, gain, table, gate_up, down_proj)
-
-
-def local(
-    queries,
-    new_keys,
-    new_values,
-    key_cache,
-    value_cache,
-    cache_len,
-    residual,
-    out_proj,
-    norm_gain,
-    expert_ids,
-    route_weights,
-    slot_expert,
-    gate_up,
-    down_proj,
-):
-    x = lax.axis_index("grp")
-    ep = lax.axis_index("ep")
-    context = jnp.concatenate(
-        [
-            prefill_context(queries, new_keys, new_values),
-            decode_context(queries, new_keys, new_values, key_cache, value_cache, cache_len),
-        ],
-        axis=0,
+    )(
+        queries,
+        new_keys,
+        new_values,
+        key_cache,
+        value_cache,
+        cache_len,
+        residual,
+        out_proj,
+        norm_gain[None, :],
+        expert_ids,
+        route_weights,
+        slot_expert[None, :],
+        gate_up,
+        down_proj,
     )
-    ctx = jnp.concatenate([context[:, :D], context[:, D:]], axis=0)
-    lane = jnp.arange(HALF)[None, :] - x * DEV_ROWS
-    spread = (lane == jnp.arange(DEV_ROWS)[:, None]).astype(BF16)
-    both = jnp.concatenate([(expert_ids + 1).astype(BF16), route_weights], axis=1)
-    meta = lax.dot_general(
-        both, spread, (((0,), (0,)), ((), ())), preferred_element_type=F32
-    ).astype(BF16)
-    quarters = residual.reshape(DEV_ROWS, NX, DQ).transpose(1, 0, 2)
-    quarters = jnp.pad(quarters, ((0, 0), (0, 8), (0, 0)))
-    meta = jnp.broadcast_to(jnp.pad(meta, ((0, 0), (0, DQ - HALF)))[None], (NX, 16, DQ))
-    side = jnp.concatenate([quarters, meta], axis=1)
-    place = ep * SLOTS_DEV + jnp.arange(SLOTS_DEV)
-    mine = lax.dynamic_slice_in_dim(slot_expert, ep * SLOTS_DEV, SLOTS_DEV)
-    same = slot_expert[None, :] == mine[:, None]
-    twice = jnp.sum(same, axis=1) > 1
-    earlier = jnp.sum(same & (jnp.arange(slot_expert.shape[0])[None, :] < place[:, None]), axis=1)
-    table = jnp.concatenate([mine + 1, twice.astype(jnp.int32), earlier, jnp.zeros((7,), jnp.int32)])
-    table = jnp.broadcast_to(table.astype(F32)[:, None], (16, 128))
-    return whole_layer(ctx, side, out_proj, norm_gain[None, :], table, gate_up, down_proj)
 
 
 def solution(mesh):

time: 157 us -> 151 us (0.962)
  Pallas kernels: 138 us -> 145 us
  matrix products: 5.54 us -> 0 us
  other arithmetic: 5.01 us -> 0 us
    pallas_call x1, Pallas kernels: 138 us -> 145 us  [local(): pl.pallas_call(layer_kernel, out_shape=(jax.ShapeDtypeStruct((DEV_ROWS, D...]
    dot_general x5 -> x0, matrix products: 4.42 us -> none  [the longest x1 1.73 us: decode_context(): jnp.einsum('nkgd,ntkd->nkgt', query_dec, cached_keys, preferred_element_t...]
    unnamed x12 -> x4, local copies, waits for them, and re-layouts: 4.93 us -> 5.78 us
where the time goes in v4:
time: 151 us
  Pallas kernels  145 us (96%)
  local copies, waits for them, and re-layouts  5.78 us (4%)
    pallas_call x1, Pallas kernels, local(): pl.pallas_call(layer_kernel, out_shape=(jax.ShapeDtypeStruct((DEV_ROWS, D...  145 us
    unnamed x4, local copies, waits for them, and re-layouts  5.78 us

profile of v4, /device:TPU:32, one launch (start us, length us, event | category | flops | bytes accessed | tf_op | source)
XLA Modules:
  0.0 151.1 jit_solution(8041232800172643566)
XLA Ops:
  0.6 1.3 copy.17.weights_ref
  2.0 1.4 copy.16.ids_ref
  3.3 144.7 %shard_map.149 = (bf16[24,2048]{1,0:T(8,128)(2,1)}, bf16[24,2048]{1,0:T(8,128)(2,1)}) custom-call(bf16[24,4096]{1,0:T(8,128)(2,1)} %queries_hbm.1, bf16[24,512]{1,0:T(8,128)(2,1)} %new_keys_hbm.1, bf16[24,512]{1,0:T(8,128)(2,1)} %new_values_hbm.1, bf16[16,48,512]{2,1,0:T(8,128)(2,1)} %key_cache_hbm.1, bf16[16,48,512]{2,1,0:T(8,128)(2,1)} %value_cache_hbm.1, ...), custom_call_target="tpu_custom_call" | custom-call | tf_op jit(solution)/shard_map/pallas_call | solution.py:700
  148.0 1.5 %copy.20 = bf16[24,2048]{1,0:T(8,128)(2,1)} copy(bf16[24,2048]{1,0:T(8,128)(2,1)} %get-tuple-element.4) | data formatting | bytes 196608
  149.5 1.5 %copy.21 = bf16[24,2048]{1,0:T(8,128)(2,1)} copy(bf16[24,2048]{1,0:T(8,128)(2,1)} %get-tuple-element.5) | data formatting | bytes 196608

commit v5 on v4

--- a/solution.py
+++ b/solution.py
@@ -43,10 +43,11 @@
 S1_R, S1_L, S2_R, S2_L = 52, 60, 68, 76
 H1_R, H1_L, H2_R, H2_L = 84, 92, 100, 108
 CORE_MIX = 116
-CHAIN = 124
-Y_SUM = 152
-FINAL = 155
-COPIES = 158
+CHAIN = 148
+Y_SUM = 176
+FINAL = 179
+CTX_LATE_R, CTX_LATE_L = 182, 183
+COPIES = 184
 
 NEAR = (2, -1, 1, 0)
 FAR = (4, -3, 3, -2)
@@ -166,21 +167,20 @@
         before = jnp.sum(jnp.where(slot_lane < here, same, 0.0), axis=1, keepdims=True)
         for row, value in ((j, mine + 1.0), (3 + j, twice), (6 + j, before)):
             table_ref[row : row + 1, :] = jnp.broadcast_to(value, (1, 128))
-    spread_row = lax.broadcasted_iota(jnp.int32, (DEV_ROWS, HALF), 0)
-    spread_lane = lax.broadcasted_iota(jnp.int32, (DEV_ROWS, HALF), 1)
+    spread_row = lax.broadcasted_iota(jnp.int32, (DEV_ROWS, 128), 0)
+    spread_lane = lax.broadcasted_iota(jnp.int32, (DEV_ROWS, 128), 1)
     to_lane = jnp.where(spread_lane == spread_row + x * DEV_ROWS, 1.0, 0.0).astype(BF16)
     routes = [
-        lax.dot_general(
-            value.astype(BF16), to_lane, (((0,), (0,)), ((), ())), preferred_element_type=F32
-        )
+        jnp.dot(value.astype(BF16), to_lane, preferred_element_type=F32)
         for value in (ids_ref[...].astype(F32) + 1.0, weights_ref[...].astype(F32))
     ]
-    routes = jnp.concatenate(routes, axis=0).astype(BF16)
+    routes = jnp.concatenate(routes, axis=1)
     for load in early:
         load.wait()
     for g in range(NX):
-        side_out[g, 0:DEV_ROWS, :] = residual[:, g * DQ : (g + 1) * DQ]
-        side_out[g, 32:48, 0:HALF] = routes
+        quarter = residual[:, g * DQ : (g + 1) * DQ].astype(F32)
+        routes_wide = jnp.concatenate([routes, jnp.zeros((TOPK, DQ - HALF), F32)], axis=1)
+        side_out[g] = jnp.concatenate([quarter, routes_wide], axis=0).astype(BF16)
 
     own_keys[...] = new_keys[...].astype(F32)
     own_values[...] = new_values[...].astype(F32)
@@ -268,22 +268,27 @@
         pending.append(made)
         return made
 
-    ctx_r = send(ctx_all.at[x], ctx_all.at[x], CTX_R, x_dev(1))
-    ctx_l = send(ctx_all.at[x], ctx_all.at[x], CTX_L, x_dev(3))
+    low, high = pl.ds(0, D // 2), pl.ds(D // 2, D // 2)
+
+    def context_part(owner, lanes, index, device):
+        part = ctx_all.at[owner, :, lanes]
+        return send(part, part, index, device)
+
     sides = []
     for step in (1, 2, 3):
         there = (x + step) % NX
         sides.append(send(side_out.at[there], side_all.at[x], SIDE + step - 1, x_dev(step)))
+    first_r = context_part(x, low, CTX_R, x_dev(1))
+    first_l = context_part(x, high, CTX_L, x_dev(3))
+    later_r = context_part(x, high, CTX_LATE_R, x_dev(1))
+    later_l = context_part(x, low, CTX_LATE_L, x_dev(3))
     from_l, from_r = (x + 3) % NX, (x + 1) % NX
-    ctx_r.wait_recv()
-    low, high = pl.ds(0, D // 2), pl.ds(D // 2, D // 2)
-    fwd_r = send(
-        ctx_all.at[from_l, :, low], ctx_all.at[from_l, :, low], CTX_FR, x_dev(1)
-    )
-    ctx_l.wait_recv()
-    fwd_l = send(
-        ctx_all.at[from_r, :, high], ctx_all.at[from_r, :, high], CTX_FL, x_dev(3)
-    )
+    first_r.wait_recv()
+    fwd_r = context_part(from_l, low, CTX_FR, x_dev(1))
+    first_l.wait_recv()
+    fwd_l = context_part(from_r, high, CTX_FL, x_dev(3))
+    later_r.wait_recv()
+    later_l.wait_recv()
     loads[0].wait()
     for side in sides:
         side.wait_recv()
@@ -296,9 +301,9 @@
     for g in range(NX):
         base = g * 2 * DEV_ROWS
         term = first[base : base + DEV_ROWS] + second[base + DEV_ROWS : base + 2 * DEV_ROWS]
-        residual = side_all[g, 0:32, :].astype(F32)[0:DEV_ROWS]
+        kept = side_all[g].astype(F32)[0:DEV_ROWS]
         attended[g * DEV_ROWS : (g + 1) * DEV_ROWS, :] = (
-            (residual + term).astype(BF16).astype(F32)
+            (kept + term).astype(BF16).astype(F32)
         )
     att = attended[...]
     total = jnp.sum(att * att, axis=1, keepdims=True)
@@ -307,13 +312,14 @@
         send(squares.at[x], squares.at[x], SQUARES + step - 1, x_dev(step)) for step in (1, 2, 3)
     ]
     meta = (
-        side_all[0, 32:48, 0:HALF].astype(F32)
-        + side_all[1, 32:48, 0:HALF].astype(F32)
-        + side_all[2, 32:48, 0:HALF].astype(F32)
-        + side_all[3, 32:48, 0:HALF].astype(F32)
+        side_all[0].astype(F32)[DEV_ROWS:]
+        + side_all[1].astype(F32)[DEV_ROWS:]
+        + side_all[2].astype(F32)[DEV_ROWS:]
+        + side_all[3].astype(F32)[DEV_ROWS:]
     )
-    rows[core, y, z, COL_ROWS : COL_ROWS + 16, 0:HALF] = meta.astype(BF16)
-    rows[core, y, z, COL_ROWS : COL_ROWS + 16, HALF:DQ] = jnp.zeros((16, HALF), BF16)
+    meta = jnp.concatenate([meta[:, 0:128], meta[:, 128:256]], axis=0)
+    meta = jnp.concatenate([meta, jnp.zeros((16, DQ - 128), F32)], axis=1)
+    rows[core, y, z, COL_ROWS : COL_ROWS + 16, :] = meta.astype(BF16)
     for share in shares:
         share.wait_recv()
     total = squares[0][:, 0:1] + squares[1][:, 0:1] + squares[2][:, 0:1] + squares[3][:, 0:1]
@@ -359,8 +365,8 @@
             copy(hidden.at[k, from_r, :, far], hidden.at[k, from_r, :, far], H2_L + k, x_dev(3)),
         )
 
-    def core_copy(k):
-        return copy(mixed.at[k, 1 - core], core_in.at[k], CORE_MIX + k, partner)
+    def core_copy(k, o):
+        return copy(mixed.at[k, 1 - core, o], core_in.at[k, o], CORE_MIX + 4 * k + o, partner)
 
     row_iota = lax.broadcasted_iota(jnp.int32, (COL_ROWS, COL_ROWS), 0)
     lane_iota = lax.broadcasted_iota(jnp.int32, (COL_ROWS, COL_ROWS), 1)
@@ -460,7 +466,8 @@
                 preferred_element_type=F32,
             )
             mixed[k, cc, column // 2] = mixture.astype(BF16)
-        core_copy(k).start()
+            if cc == 1:
+                core_copy(k, column // 2).start()
 
     def chunk_with(group, offset):
         near = offset in NEAR
@@ -480,6 +487,8 @@
 
     def block(group, offset):
         k, index = chunk_with(group, offset)
+        if k == NZ - 1:
+            core_copy(k, index).wait_recv()
         return mixed[k, core, index].astype(F32) + core_in[k, index].astype(F32)
 
     def chain(group, step):
@@ -609,10 +618,11 @@
                     work()
 
     def core_arrived(k):
-        core_copy(k).wait_recv()
+        for o in range(4):
+            core_copy(k, o).wait_recv()
 
     def tick(t, carry):
-        pl.when((t >= 5) & (t < NZ + 5))(functools.partial(core_arrived, t - 5))
+        pl.when((t >= 5) & (t < NZ + 4))(functools.partial(core_arrived, t - 5))
         at(t, chains)
         for stage, work in ((4, mix), (3, pass_hidden), (2, add_second), (1, add_first)):
             pl.when((t >= stage) & (t < NZ + stage))(functools.partial(work, t - stage))
@@ -651,7 +661,7 @@
             *second_copies(k),
             *hidden_copies(k),
             *forward_copies(k),
-            core_copy(k),
+            *(core_copy(k, o) for o in range(4)),
         ):
             made.wait_send()
 
@@ -717,9 +727,9 @@
             pltpu.VMEM((DEV_ROWS, width), F32),
             pltpu.VMEM((DEV_ROWS, width), F32),
             pltpu.VMEM((16, 128), F32),
-            pltpu.VMEM((NX, 48, DQ), BF16),
+            pltpu.VMEM((NX, 32, DQ), BF16),
             pltpu.VMEM((NX, 2 * DEV_ROWS, D), BF16),
-            pltpu.VMEM((NX, 48, DQ), BF16),
+            pltpu.VMEM((NX, 32, DQ), BF16),
             pltpu.VMEM((2 * D, DQ), BF16),
             pltpu.VMEM((SLOTS_DEV, DQ, 2 * FF), BF16),
             pltpu.VMEM((SLOTS_DEV, FF, DQ), BF16),
@@ -758,8 +768,8 @@
         residual,
         out_proj,
         norm_gain[None, :],
-        expert_ids,
-        route_weights,
+        expert_ids.T,
+        route_weights.T,
         slot_expert[None, :],
         gate_up,
         down_proj,

time: 151 us -> 148 us (0.980)
  local copies, waits for them, and re-layouts: 5.78 us -> 3.08 us
    unnamed x4 -> x2, local copies, waits for them, and re-layouts: 5.78 us -> 3.08 us
where the time goes in v5:
time: 148 us
  Pallas kernels  144 us (97%)
  local copies, waits for them, and re-layouts  3.08 us (2%)
    pallas_call x1, Pallas kernels, local(): pl.pallas_call(layer_kernel, out_shape=(jax.ShapeDtypeStruct((DEV_ROWS, D...  144 us
    unnamed x2, local copies, waits for them, and re-layouts  3.08 us

profile of v5, /device:TPU:32, one launch (start us, length us, event | category | flops | bytes accessed | tf_op | source)
XLA Modules:
  0.0 147.6 jit_solution(9636880090569380777)
XLA Ops:
  0.6 143.9 %shard_map.149 = (bf16[24,2048]{1,0:T(8,128)(2,1)}, bf16[24,2048]{1,0:T(8,128)(2,1)}) custom-call(bf16[24,4096]{1,0:T(8,128)(2,1)} %queries_hbm.1, bf16[24,512]{1,0:T(8,128)(2,1)} %new_keys_hbm.1, bf16[24,512]{1,0:T(8,128)(2,1)} %new_values_hbm.1, bf16[16,48,512]{2,1,0:T(8,128)(2,1)} %key_cache_hbm.1, bf16[16,48,512]{2,1,0:T(8,128)(2,1)} %value_cache_hbm.1, ...), custom_call_target="tpu_custom_call" | custom-call | tf_op jit(solution)/shard_map/pallas_call | solution.py:710
  144.6 1.5 %copy.18 = bf16[24,2048]{1,0:T(8,128)(2,1)} copy(bf16[24,2048]{1,0:T(8,128)(2,1)} %get-tuple-element.4) | data formatting | bytes 196608
  146.1 1.5 %copy.19 = bf16[24,2048]{1,0:T(8,128)(2,1)} copy(bf16[24,2048]{1,0:T(8,128)(2,1)} %get-tuple-element.5) | data formatting | bytes 196608

commit v6 on v5

--- a/solution.py
+++ b/solution.py
@@ -68,8 +68,7 @@
     slots_ref,
     gate_up_hbm,
     down_hbm,
-    moe_ref,
-    layer_ref,
+    result_ref,
     queries,
     new_keys,
     new_values,
@@ -650,10 +649,7 @@
     for made in finals:
         made.wait_recv()
     for g in range(NX):
-        ended = final_in[g].astype(F32)
-        lanes = slice(g * DQ, (g + 1) * DQ)
-        moe_ref[:, lanes] = ended[0:DEV_ROWS].astype(BF16)
-        layer_ref[:, lanes] = ended[DEV_ROWS : 2 * DEV_ROWS].astype(BF16)
+        result_ref[:, g * DQ : (g + 1) * DQ] = final_in[g]
 
     def drain(k, carry):
         for made in (
@@ -707,14 +703,11 @@
     smem = pl.BlockSpec(memory_space=pltpu.SMEM)
     hbm = pl.BlockSpec(memory_space=pl.ANY)
     requests, cached, width = key_cache.shape
-    return pl.pallas_call(
+    both = pl.pallas_call(
         layer_kernel,
-        out_shape=(
-            jax.ShapeDtypeStruct((DEV_ROWS, D), BF16),
-            jax.ShapeDtypeStruct((DEV_ROWS, D), BF16),
-        ),
+        out_shape=jax.ShapeDtypeStruct((2 * DEV_ROWS, D), BF16),
         in_specs=[hbm] * 5 + [smem] + [hbm] * 2 + [vmem] * 4 + [hbm] * 2,
-        out_specs=(vmem, vmem),
+        out_specs=vmem,
         scratch_shapes=[
             pltpu.VMEM((DEV_ROWS, 2 * D), BF16),
             pltpu.VMEM((DEV_ROWS, width), BF16),
@@ -774,6 +767,7 @@
         gate_up,
         down_proj,
     )
+    return both[:DEV_ROWS], both[DEV_ROWS:]
 
 
 def solution(mesh):

time: 148 us -> 146 us (0.986)
    unnamed x2 -> x0, local copies, waits for them, and re-layouts: 3.08 us -> none
    slice x0 -> x1, local copies, waits for them, and re-layouts: none -> 1.63 us  [local(): return (both[:DEV_ROWS], both[DEV_ROWS:])]
where the time goes in v6:
time: 146 us
  Pallas kernels  144 us (99%)
  local copies, waits for them, and re-layouts  1.63 us (1%)
    pallas_call x1, Pallas kernels, local(): pl.pallas_call(layer_kernel, out_shape=jax.ShapeDtypeStruct((2 * DEV_ROWS...  144 us

profile of v6, /device:TPU:32, one launch (start us, length us, event | category | flops | bytes accessed | tf_op | source)
XLA Modules:
  0.0 146.2 jit_solution(17085185397572176077)
XLA Ops:
  0.6 143.9 %shard_map.149 = bf16[48,2048]{1,0:T(8,128)(2,1)} custom-call(bf16[24,4096]{1,0:T(8,128)(2,1)} %queries_hbm.1, bf16[24,512]{1,0:T(8,128)(2,1)} %new_keys_hbm.1, bf16[24,512]{1,0:T(8,128)(2,1)} %new_values_hbm.1, bf16[16,48,512]{2,1,0:T(8,128)(2,1)} %key_cache_hbm.1, bf16[16,48,512]{2,1,0:T(8,128)(2,1)} %value_cache_hbm.1, s32[16]{0:T(128)} %cache_len_ref.1, ...), custom_call_target="tpu_custom_call" | custom-call | tf_op jit(solution)/shard_map/pallas_call | solution.py:706
  144.5 1.6 %fusion = (bf16[24,2048]{1,0:T(8,128)(2,1)}, bf16[24,2048]{1,0:T(8,128)(2,1)}) fusion(bf16[48,2048]{1,0:T(8,128)(2,1)} %shard_map.149), kind=kLoop, calls=%fused_computation | loop fusion | bytes 393216 | tf_op jit(solution)/shard_map/slice | solution.py:770

commit v7 on v6

--- a/solution.py
+++ b/solution.py
@@ -273,12 +273,12 @@
         part = ctx_all.at[owner, :, lanes]
         return send(part, part, index, device)
 
+    first_r = context_part(x, low, CTX_R, x_dev(1))
+    first_l = context_part(x, high, CTX_L, x_dev(3))
     sides = []
     for step in (1, 2, 3):
         there = (x + step) % NX
         sides.append(send(side_out.at[there], side_all.at[x], SIDE + step - 1, x_dev(step)))
-    first_r = context_part(x, low, CTX_R, x_dev(1))
-    first_l = context_part(x, high, CTX_L, x_dev(3))
     later_r = context_part(x, high, CTX_LATE_R, x_dev(1))
     later_l = context_part(x, low, CTX_LATE_L, x_dev(3))
     from_l, from_r = (x + 3) % NX, (x + 1) % NX

time: 146 us -> 147 us (level)
  no operation moved by 1% of the time
where the time goes in v7:
time: 147 us
  Pallas kernels  145 us (99%)
  local copies, waits for them, and re-layouts  1.63 us (1%)
    pallas_call x1, Pallas kernels, local(): pl.pallas_call(layer_kernel, out_shape=jax.ShapeDtypeStruct((2 * DEV_ROWS...  145 us

profile of v7, /device:TPU:32, one launch (start us, length us, event | category | flops | bytes accessed | tf_op | source)
XLA Modules:
  0.0 146.9 jit_solution(4333736153800142688)
XLA Ops:
  0.6 144.7 %shard_map.149 = bf16[48,2048]{1,0:T(8,128)(2,1)} custom-call(bf16[24,4096]{1,0:T(8,128)(2,1)} %queries_hbm.1, bf16[24,512]{1,0:T(8,128)(2,1)} %new_keys_hbm.1, bf16[24,512]{1,0:T(8,128)(2,1)} %new_values_hbm.1, bf16[16,48,512]{2,1,0:T(8,128)(2,1)} %key_cache_hbm.1, bf16[16,48,512]{2,1,0:T(8,128)(2,1)} %value_cache_hbm.1, s32[16]{0:T(128)} %cache_len_ref.1, ...), custom_call_target="tpu_custom_call" | custom-call | tf_op jit(solution)/shard_map/pallas_call | solution.py:706
  145.3 1.6 %fusion = (bf16[24,2048]{1,0:T(8,128)(2,1)}, bf16[24,2048]{1,0:T(8,128)(2,1)}) fusion(bf16[48,2048]{1,0:T(8,128)(2,1)} %shard_map.149), kind=kLoop, calls=%fused_computation | loop fusion | bytes 393216 | tf_op jit(solution)/shard_map/slice | solution.py:770
